TPU v7x, 32 devices: a whole 2x2x4 slice. The times are simulated.
32 devices in a mesh: row: 4 (over y, x), col: 8 (over z, core).
Axes of the slice: x: 2, y: 2, z: 4, core: 2. Of those that a mesh axis runs over, the one named last changes fastest.
Arguments:
- tokens: bfloat16 [128, 512, 192], P('row', 'col'), may hold values from -6 to 6
- norm_gain: float32 [2, 3, 192], replicated, may hold values from 0.1 to 1.9
- qkv_weight: bfloat16 [2, 192, 576], replicated, may hold values from -0.4375 to 0.4375
- proj_weight: bfloat16 [2, 192, 192], replicated, may hold values from -0.4375 to 0.4375
- bias_table: float32 [2, 6, 225], replicated, may hold values from -4 to 4
- conv_weight: float32 [2, 49, 192], replicated, may hold values from -0.875 to 0.875
- up_weight: bfloat16 [2, 192, 768], replicated, may hold values from -0.4375 to 0.4375
- down_weight: bfloat16 [2, 768, 192], replicated, may hold values from -0.21875 to 0.21875
Outputs:
- mixed: bfloat16 [128, 512, 192], P('row', 'col')
All inputs are finite; a program needn't handle non-finite values.
Results may differ from a plain program's by a relative error of at most 0.013.
Values may be sent and summed in bfloat16 or wider, within the bound.
A program may use at most 64 MiB of HBM per device.

v0:
```python
import functools

import jax
import jax.numpy as jnp
from jax import lax
from jax.experimental import pallas as pl
from jax.experimental.pallas import tpu as pltpu
from jax.sharding import PartitionSpec as P

D = 192
HEADS = 6
WS = 8
KS = 7
LAYERS = 2
HEAD = 32
AREA = WS * WS
HALO = KS // 2

epsilon = 1e-05
LOG2E = 1.4426950408889634
VALUE_SCALE = 2.0**-8
EXP_CAP = 3.3895313892515355e38


def padded_2(cells, sides, width):
    for axis, dim in sides:
        count = lax.axis_size(axis)
        ends = count - 1
        head = lax.slice_in_dim(cells, 0, width, axis=dim)
        tail = lax.slice_in_dim(cells, cells.shape[dim] - width, cells.shape[dim], axis=dim)
        cells = jnp.concatenate(
            [
                lax.ppermute(tail, axis, [(i, (i + 1) % count) for i in range(ends)]),
                cells,
                lax.ppermute(head, axis, [((i + 1) % count, i) for i in range(ends)]),
            ],
            axis=dim,
        )
    return cells


def norm(values, gain):
    centre = jnp.mean(values, axis=-1, keepdims=True)
    centred = values - centre
    spread = jnp.mean(centred * centred, axis=-1, keepdims=True)
    return centred * lax.rsqrt(spread + epsilon) * gain


def score_bias(lookup_table):
    places = jnp.arange(AREA, dtype=jnp.int32)
    row, col = places // WS, places % WS
    offsets = (row[:, None] - row[None, :] + WS - 1) * (2 * WS - 1) + (
        col[:, None] - col[None, :] + WS - 1
    )
    entries = jnp.arange((2 * WS - 1) * (2 * WS - 1), dtype=jnp.int32)
    selector = (offsets.reshape(-1)[:, None] == entries[None, :]).astype(jnp.float32)
    expanded = jnp.dot(lookup_table, selector.T, precision=lax.Precision.HIGHEST) * LOG2E
    return expanded.reshape(HEADS, AREA, AREA).transpose(1, 0, 2).reshape(AREA, HEADS * AREA)


def attention(normed, qkv_ref, proj_ref, bias_ref):
    count = normed.shape[0] // AREA
    query, key, value = (
        jnp.dot(normed, qkv_ref[part], preferred_element_type=jnp.float32).astype(jnp.bfloat16)
        for part in range(3)
    )
    lane_head = lax.broadcasted_iota(jnp.int32, (1, D), 1) // HEAD
    masks = [(lane_head == head).astype(jnp.bfloat16) for head in range(HEADS)]
    value_masks = [mask * VALUE_SCALE for mask in masks]
    sums = jnp.concatenate([jnp.broadcast_to(mask, (AREA, D)) for mask in value_masks], axis=0)
    bias = bias_ref[...]
    outs, exps = [], []
    for window in range(count):
        rows = slice(window * AREA, (window + 1) * AREA)
        keys = jnp.concatenate([key[rows] * mask for mask in masks], axis=0)
        scores = lax.dot_general(
            query[rows], keys, (((1,), (1,)), ((), ())), preferred_element_type=jnp.float32
        )
        exped = jnp.minimum(jnp.exp2(scores * (HEAD**-0.5 * LOG2E) + bias), EXP_CAP)
        exped = exped.astype(jnp.bfloat16)
        values = jnp.concatenate([value[rows] * mask for mask in value_masks], axis=0)
        outs.append(jnp.dot(exped, values, preferred_element_type=jnp.float32))
        exps.append(exped)
    total = jnp.dot(jnp.concatenate(exps, axis=0), sums, preferred_element_type=jnp.float32)
    attended = (jnp.concatenate(outs, axis=0) / total).astype(jnp.bfloat16)
    branch = jnp.dot(attended, proj_ref[...], preferred_element_type=jnp.float32)
    return branch.astype(jnp.bfloat16).astype(jnp.float32)


def regular_kernel(x_ref, gain_ref, qkv_ref, proj_ref, bias_ref, after_ref, normed_ref):
    rows, width = x_ref.shape[0], x_ref.shape[1]
    current = x_ref[...].astype(jnp.float32)
    normed = norm(current.reshape(rows * width, D), gain_ref[0])
    windows = normed.reshape(WS, width // WS, WS, D).transpose(1, 0, 2, 3).reshape(rows * width, D)
    branch = attention(windows.astype(jnp.bfloat16), qkv_ref, proj_ref, bias_ref)
    branch = branch.reshape(width // WS, WS, WS, D).transpose(1, 0, 2, 3).reshape(rows, width, D)
    after = current + branch
    after_ref[...] = after
    normed_ref[...] = norm(after, gain_ref[1]).astype(jnp.bfloat16)


def shuffle_kernel(x_ref, qkv_ref, proj_ref, bias_ref, out_ref):
    across = x_ref.shape[3]
    tokens = x_ref[:, 0].astype(jnp.float32)
    windows = jnp.swapaxes(tokens, 1, 2).transpose(1, 0, 2, 3).reshape(across * AREA, D)
    branch = attention(windows.astype(jnp.bfloat16), qkv_ref, proj_ref, bias_ref)
    branch = branch.reshape(across, WS, WS, D).transpose(1, 0, 2, 3)
    out_ref[:, 0] = jnp.swapaxes(branch, 1, 2).astype(jnp.bfloat16)


def residual_kernel(x_ref, branch_ref, gain_ref, after_ref, normed_ref):
    after = x_ref[...].astype(jnp.float32) + branch_ref[...].astype(jnp.float32)
    after_ref[...] = after
    normed_ref[...] = norm(after, gain_ref[1]).astype(jnp.bfloat16)


def conv_mlp_kernel(
    padded_ref, after_ref, gain_ref, taps_ref, up_ref, down_ref, *rest
):
    out_refs, (wide, taps, conv) = rest[:-3], rest[-3:]
    rows, width = after_ref.shape[0], after_ref.shape[1]
    step = pl.program_id(0)

    @pl.when(step == 0)
    def _():
        wide[:, : padded_ref.shape[1], :] = padded_ref[...].astype(jnp.float32)
        taps[...] = jnp.broadcast_to(taps_ref[...][:, None, :], taps.shape)

    base = step * rows
    for left in range(0, width, 8):
        for lanes in (slice(0, 128), slice(128, D)):
            sums = [after_ref[r, left : left + 8, lanes] for r in range(rows)]
            for v in range(KS):
                weights = [taps[u * KS + v, :, lanes] for u in range(KS)]
                for r in range(rows + KS - 1):
                    cell = wide[base + r, left + v : left + v + 8, lanes]
                    for u in range(KS):
                        if 0 <= r - u < rows:
                            sums[r - u] = sums[r - u] + cell * weights[u]
            for r in range(rows):
                conv[r, left : left + 8, lanes] = sums[r]
    flat = conv[...].reshape(rows * width, D)
    normed = norm(flat, gain_ref[2]).astype(jnp.bfloat16)
    up = jnp.dot(normed, up_ref[...], preferred_element_type=jnp.float32)
    hidden = (0.5 * up * (1.0 + lax.erf(up * 0.5**0.5))).astype(jnp.bfloat16)
    outcome = flat + jnp.dot(hidden, down_ref[...], preferred_element_type=jnp.float32)
    current = outcome.astype(jnp.bfloat16)
    out_refs[0][...] = current.reshape(rows, width, D)
    if len(out_refs) == 2:
        following = norm(current.astype(jnp.float32), gain_ref[3])
        out_refs[1][...] = following.astype(jnp.bfloat16).reshape(rows, width, D)


def whole(shape):
    return pl.BlockSpec(shape, lambda i: (0,) * len(shape))


def stripe(width):
    return pl.BlockSpec((WS, width, D), lambda i: (i, 0, 0))


def shuffled(normed, qkv, proj, bias):
    height, width = normed.shape[0], normed.shape[1]
    row_count, col_count = lax.axis_size("row"), lax.axis_size("col")
    row_repeat, col_repeat = max(1, WS // row_count), max(1, WS // col_count)
    row_piece = height // row_repeat // row_count
    col_piece = width // col_repeat // col_count
    layout = normed.reshape(row_repeat, row_count, row_piece, col_repeat, col_count, col_piece, D)
    outgoing = layout.transpose(1, 4, 0, 2, 3, 5, 6).reshape(
        row_count * col_count, row_repeat, row_piece, col_repeat, col_piece, D
    )
    received = lax.all_to_all(outgoing, ("row", "col"), split_axis=0, concat_axis=0, tiled=True)
    grid = received.reshape(
        row_count, col_count, row_repeat, row_piece, col_repeat, col_piece, D
    ).transpose(0, 2, 3, 1, 4, 5, 6)
    down = row_count * row_repeat * row_piece // WS
    across = col_count * col_repeat * col_piece // WS
    grid = grid.reshape(WS, down, WS, across, D)
    block = pl.BlockSpec((WS, 1, WS, across, D), lambda i: (0, i, 0, 0, 0))
    result = pl.pallas_call(
        shuffle_kernel,
        out_shape=jax.ShapeDtypeStruct(grid.shape, jnp.bfloat16),
        grid=(down,),
        in_specs=[block, whole(qkv.shape), whole(proj.shape), whole(bias.shape)],
        out_specs=block,
        name="shuffle_attention",
    )(grid, qkv, proj, bias)
    result = result.reshape(
        row_count, row_repeat, row_piece, col_count, col_repeat, col_piece, D
    ).transpose(0, 3, 1, 2, 4, 5, 6)
    result = result.reshape(row_count * col_count, row_repeat, row_piece, col_repeat, col_piece, D)
    returned = lax.all_to_all(result, ("row", "col"), split_axis=0, concat_axis=0, tiled=True)
    returned = returned.reshape(
        row_count, col_count, row_repeat, row_piece, col_repeat, col_piece, D
    ).transpose(2, 0, 3, 4, 1, 5, 6)
    return returned.reshape(height, width, D)


def on_device(
    tokens, norm_gain, qkv_weight, proj_weight, bias_table, conv_weight, up_weight, down_weight
):
    height, width = tokens.shape[0], tokens.shape[1]
    shape32 = jax.ShapeDtypeStruct(tokens.shape, jnp.float32)
    shape16 = jax.ShapeDtypeStruct(tokens.shape, jnp.bfloat16)
    qkv_parts = qkv_weight.reshape(LAYERS, D, 3, D).transpose(0, 2, 1, 3)
    current, normed = tokens, None
    for layer in range(LAYERS):
        bias = score_bias(bias_table[layer])
        gains = norm_gain[layer][:, None, :]
        qkv, proj = qkv_parts[layer], proj_weight[layer]
        if layer % 2 == 0:
            after, normed_two = pl.pallas_call(
                regular_kernel,
                out_shape=(shape32, shape16),
                grid=(height // WS,),
                in_specs=[
                    stripe(width),
                    whole(gains.shape),
                    whole(qkv.shape),
                    whole(proj.shape),
                    whole(bias.shape),
                ],
                out_specs=(stripe(width), stripe(width)),
                name="regular_attention",
            )(current, gains, qkv, proj, bias)
        else:
            branch = shuffled(normed, qkv, proj, bias)
            after, normed_two = pl.pallas_call(
                residual_kernel,
                out_shape=(shape32, shape16),
                grid=(height // WS,),
                in_specs=[stripe(width), stripe(width), whole(gains.shape)],
                out_specs=(stripe(width), stripe(width)),
                name="residual",
            )(current, branch, gains)
        padded = padded_2(normed_two, (("row", 0), ("col", 1)), HALO)
        last = layer == LAYERS - 1
        if not last:
            gains = jnp.concatenate([gains, norm_gain[layer + 1, :1][:, None, :]], axis=0)
        outs = pl.pallas_call(
            conv_mlp_kernel,
            out_shape=(shape16,) if last else (shape16, shape16),
            grid=(height // WS,),
            in_specs=[
                whole(padded.shape),
                stripe(width),
                whole(gains.shape),
                whole((KS * KS, D)),
                whole(up_weight.shape[1:]),
                whole(down_weight.shape[1:]),
            ],
            out_specs=(stripe(width),) if last else (stripe(width), stripe(width)),
            scratch_shapes=[
                pltpu.VMEM((padded.shape[0], -(-padded.shape[1] // 8) * 8, D), jnp.float32),
                pltpu.VMEM((KS * KS, 8, D), jnp.float32),
                pltpu.VMEM((WS, width, D), jnp.float32),
            ],
            name="conv_mlp",
        )(padded, after, gains, conv_weight[layer], up_weight[layer], down_weight[layer])
        current = outs[0]
        normed = None if last else outs[1]
    return current


def solution(mesh):
    in_specs = (P("row", "col", None), P(), P(), P(), P(), P(), P(), P())
    return jax.shard_map(
        on_device, mesh=mesh, in_specs=in_specs, out_specs=P("row", "col", None), check_vma=False
    )
```

profile of v0, /device:TPU:1, one launch (start us, length us, event | category | flops | bytes accessed | tf_op | source)
XLA Modules:
  0.0 193.0 jit_solution(17552249705541852095)
XLA Ops:
  0.0 0.1 add_add_fusion
  0.1 0.1 add.66
  0.2 0.8 fusion.10
  1.0 2.0 %fusion.1 = f32[6,4096]{1,0:T(8,128)S(1)} fusion(s32[4096]{0:T(1024)S(1)} %add.66, f32[1,6,225]{2,0,1:T(1,128)S(1)} %get-tuple-element.36), kind=kOutput, calls=%fused_computation.3 | convolution fusion | flops 67301376 | bytes 120088 | tf_op jit(solution)/shard_map/dot_general | solution.py:57
  3.0 0.1 reshape.123
  3.1 0.1 copy.64
  3.2 0.7 reshape.124.bias_ref
  3.9 0.0 copy-done.7
  3.9 0.6 slice_bitcast_fusion.6
  4.6 0.0 copy-done.3
  4.6 0.2 copy.31
  4.8 0.0 copy-start.4
  4.8 0.3 copy.32
  5.1 0.9 slice_bitcast_fusion
  6.0 0.7 slice_bitcast_fusion.4
  6.7 11.7 %regular_attention.1 = (f32[32,64,192]{2,1,0:T(8,128)}, bf16[32,64,192]{2,1,0:T(8,128)(2,1)}) custom-call(bf16[32,64,192]{2,1,0:T(8,128)(2,1)} %x_ref.1, f32[3,1,192]{2,1,0:T(1,128)} %get-tuple-element.38.gain_ref, bf16[3,192,192]{2,1,0:T(8,128)(2,1)} %get-tuple-element.30.qkv_ref, bf16[192,192]{1,0:T(8,128)(2,1)} %get-tuple-element.32.proj_ref, ...), custom_call_target="tpu_custom_call" | custom-call | tf_op jit(solution)/shard_map/regular_attention/pallas_call | solution.py:212
  18.4 1.0 fusion.7
  19.4 0.0 copy-start
  19.4 4.1 %collective-permute-start = (bf16[3,64,192]{2,1,0:T(8,128)(2,1)S(1)}, bf16[3,64,192]{2,1,0:T(8,128)(2,1)S(1)}, u32[]{:S(2)}, u32[]{:S(2)}) collective-permute-start(bf16[3,64,192]{2,1,0:T(8,128)(2,1)S(1)} %get-tuple-element.24), channel_id=1, source_target_pairs={{0,8},{8,16},{16,24},{1,9},{9,17},{17,25},{2,10},{10,18},{18,26},{... | collective-permute-start | bytes 221192 | tf_op jit(solution)/shard_map/ppermute | solution.py:33
  23.5 1.3 collective-permute-start.1
  24.8 0.9 slice_bitcast_fusion.2
  25.7 0.0 copy-done.5
  25.7 0.1 fusion.9
  25.8 0.0 collective-permute-done
  25.9 0.1 constant_dynamic-update-slice_fusion.1
  26.0 2.9 %collective-permute-done.1 = bf16[3,64,192]{2,1,0:T(8,128)(2,1)S(1)} collective-permute-done((bf16[3,64,192]{2,1,0:T(8,128)(2,1)S(1)}, bf16[3,64,192]{2,1,0:T(8,128)(2,1)S(1)}, u32[]{:S(2)}, u32[]{:S(2)}) %collective-permute-start.1) | collective-permute-done | bytes 73760 | tf_op jit(solution)/shard_map/ppermute | solution.py:35
  28.9 0.1 fusion.5
  28.9 5.2 %collective-permute-start.2 = (bf16[38,3,192]{2,1,0:T(4,128)(2,1)S(1)}, bf16[38,3,192]{2,1,0:T(4,128)(2,1)S(1)}, u32[]{:S(2)}, u32[]{:S(2)}) collective-permute-start(bf16[38,3,192]{2,1,0:T(4,128)(2,1)S(1)} %get-tuple-element.19), channel_id=1, source_target_pairs={{0,1},{1,2},{2,3},{3,4},{4,5},{5,6},{6,7},{8,9},{9,10},{10,11},{11... | collective-permute-start | bytes 131336 | tf_op jit(solution)/shard_map/ppermute | solution.py:33
  34.1 1.9 collective-permute-start.3
  36.0 0.6 pad_maximum_fusion.2.gain_ref
  36.7 0.9 copy.51
  37.6 0.6 copy.66
  38.2 0.0 collective-permute-done.2
  38.2 1.6 collective-permute-done.3
  39.8 1.8 pad_maximum_fusion.padded_ref
  41.6 25.4 %conv_mlp.2 = (bf16[32,64,192]{2,1,0:T(8,128)(2,1)}, bf16[32,64,192]{2,1,0:T(8,128)(2,1)}) custom-call(bf16[38,70,192]{2,1,0:T(8,128)(2,1)} %pad_maximum_fusion.padded_ref, f32[32,64,192]{2,1,0:T(8,128)} %get-tuple-element.12.after_ref, f32[4,1,192]{2,1,0:T(1,128)} %pad_maximum_fusion.2.gain_ref, f32[49,192]{1,0:T(8,128)} %bitcast.77, ...), custom_call_target="tpu_custom_call" | custom-call | tf_op jit(solution)/shard_map/conv_mlp/pallas_call | solution.py:240
  67.0 2.3 %copy.38 = bf16[2,4,4,1,8,8,192]{6,5,2,0,4,1,3:T(8,128)(2,1)} copy(bf16[2,4,4,1,8,8,192]{6,5,4,2,1,0,3:T(8,128)(2,1)} %bitcast.76) | data formatting | bytes 1572864 | tf_op jit(solution)/shard_map/reshape | solution.py:168
  69.4 4.7 %all-to-all-start = ((bf16[32,2,4,1,8,192]{5,4,2,1,3,0:T(8,128)(2,1)}), bf16[32,2,4,1,8,192]{5,4,2,1,3,0:T(8,128)(2,1)S(1)}, u32[]{:S(2)}, u32[]{:S(2)}) async-start(bf16[32,2,4,1,8,192]{5,4,2,1,3,0:T(8,128)(2,1)} %bitcast.14), calls=%async_computation | async-start | bytes 2097152 | tf_op jit(solution)/shard_map/all_to_all | solution.py:172
  74.0 2.0 %fusion = f32[6,4096]{1,0:T(8,128)S(1)} fusion(s32[4096]{0:T(1024)S(1)} %add.66, f32[1,6,225]{2,0,1:T(1,128)S(1)} %get-tuple-element.35), kind=kOutput, calls=%fused_computation.1 | convolution fusion | flops 67301376 | bytes 120088 | tf_op jit(solution)/shard_map/dot_general | solution.py:57
  76.0 0.1 reshape.129
  76.1 0.1 copy.63
  76.2 0.7 reshape.130.bias_ref
  77.0 24.0 %all-to-all-done = bf16[32,2,4,1,8,192]{5,4,2,1,3,0:T(8,128)(2,1)S(1)} async-done(((bf16[32,2,4,1,8,192]{5,4,2,1,3,0:T(8,128)(2,1)}), bf16[32,2,4,1,8,192]{5,4,2,1,3,0:T(8,128)(2,1)S(1)}, u32[]{:S(2)}, u32[]{:S(2)}) %all-to-all-start) | async-done | bytes 786464 | tf_op jit(solution)/shard_map/all_to_all | solution.py:172
  101.0 1.1 copy.40
  102.1 10.3 %shuffle_attention.1 = bf16[8,4,8,8,192]{4,3,2,1,0:T(8,128)(2,1)} custom-call(bf16[8,4,8,8,192]{4,3,2,1,0:T(8,128)(2,1)} %bitcast.65, bf16[3,192,192]{2,1,0:T(8,128)(2,1)} %get-tuple-element.29.qkv_ref, bf16[192,192]{1,0:T(8,128)(2,1)} %get-tuple-element.31.proj_ref, f32[64,384]{1,0:T(8,128)} %reshape.130.bias_ref), custom_call_target="tpu_custom_call" | custom-call | tf_op jit(solution)/shard_map/shuffle_attention/pallas_call | solution.py:180
  112.4 1.4 copy.43
  113.8 29.6 %all_to_all.10 = bf16[32,2,4,1,8,192]{5,4,2,1,3,0:T(8,128)(2,1)S(1)} all-to-all(bf16[32,2,4,1,8,192]{5,4,2,1,3,0:T(8,128)(2,1)S(1)} %bitcast.68), channel_id=1, replica_groups=mesh['row'=4,'col'=8] {'row','col'}, dimensions={0} | all-to-all | bytes 1572864 | tf_op jit(solution)/shard_map/all_to_all | solution.py:192
  143.4 1.1 copy.45
  144.5 4.0 %residual.1 = (f32[32,64,192]{2,1,0:T(8,128)}, bf16[32,64,192]{2,1,0:T(8,128)(2,1)}) custom-call(bf16[32,64,192]{2,1,0:T(8,128)(2,1)} %get-tuple-element.13.x_ref, bf16[32,64,192]{2,1,0:T(8,128)(2,1)} %bitcast.66, f32[3,1,192]{2,1,0:T(1,128)} %get-tuple-element.37.gain_ref), custom_call_target="tpu_custom_call" | custom-call | tf_op jit(solution)/shard_map/residual/pallas_call | solution.py:228
  148.5 1.0 fusion.6
  149.5 2.8 %collective-permute-start.4 = (bf16[3,64,192]{2,1,0:T(8,128)(2,1)S(1)}, bf16[3,64,192]{2,1,0:T(8,128)(2,1)S(1)}, u32[]{:S(2)}, u32[]{:S(2)}) collective-permute-start(bf16[3,64,192]{2,1,0:T(8,128)(2,1)S(1)} %get-tuple-element.22), channel_id=1, source_target_pairs={{0,8},{8,16},{16,24},{1,9},{9,17},{17,25},{2,10},{10,18},{18,26},{... | collective-permute-start | bytes 221192 | tf_op jit(solution)/shard_map/ppermute | solution.py:33
  152.3 1.3 collective-permute-start.5
  153.6 0.9 collective-permute-done.4
  154.6 1.3 constant_dynamic-update-slice_fusion.4
  155.9 2.9 %collective-permute-done.5 = bf16[3,64,192]{2,1,0:T(8,128)(2,1)S(1)} collective-permute-done((bf16[3,64,192]{2,1,0:T(8,128)(2,1)S(1)}, bf16[3,64,192]{2,1,0:T(8,128)(2,1)S(1)}, u32[]{:S(2)}, u32[]{:S(2)}) %collective-permute-start.5) | collective-permute-done | bytes 73760 | tf_op jit(solution)/shard_map/ppermute | solution.py:35
  158.8 0.1 fusion.4
  158.8 1.9 collective-permute-start.6
  160.8 2.4 %collective-permute-start.7 = (bf16[38,3,192]{2,1,0:T(4,128)(2,1)S(1)}, bf16[38,3,192]{2,1,0:T(4,128)(2,1)S(1)}, u32[]{:S(2)}, u32[]{:S(2)}) collective-permute-start(bf16[38,3,192]{2,1,0:T(4,128)(2,1)S(1)} %get-tuple-element.18), channel_id=1, source_target_pairs={{1,0},{2,1},{3,2},{4,3},{5,4},{6,5},{7,6},{9,8},{10,9},{11,10},{12... | collective-permute-start | bytes 131336 | tf_op jit(solution)/shard_map/ppermute | solution.py:35
  163.2 0.9 copy.54
  164.1 0.6 copy.65
  164.7 0.0 collective-permute-done.6
  164.7 1.8 collective-permute-done.7
  166.5 1.8 pad_maximum_fusion.1.padded_ref
  168.3 24.7 %conv_mlp.3 = bf16[32,64,192]{2,1,0:T(8,128)(2,1)} custom-call(bf16[38,70,192]{2,1,0:T(8,128)(2,1)} %pad_maximum_fusion.1.padded_ref, f32[32,64,192]{2,1,0:T(8,128)} %get-tuple-element.16.after_ref, f32[3,1,192]{2,1,0:T(1,128)} %get-tuple-element.37.gain_ref, f32[49,192]{1,0:T(8,128)} %bitcast.78, bf16[192,768]{1,0:T(8,128)(2,1)} %get-tuple-element.27.up_ref, ...), custom_call_target="tpu_custom_call" | custom-call | tf_op jit(solution)/shard_map/conv_mlp/pallas_call | solution.py:240
  (18 shorter events, 0.1 us)
Async XLA Ops:
  0.0 3.9 %copy-start.7 = (f32[2,3,192]{2,0,1:T(2,128)S(1)}, f32[2,3,192]{2,0,1:T(2,128)}, u32[]{:S(2)}) copy-start(f32[2,3,192]{2,0,1:T(2,128)} %param.9) | copy-start | bytes 13828
  0.0 4.6 %copy-start.3 = (bf16[2,192,576]{2,1,0:T(8,128)(2,1)S(1)}, bf16[2,192,576]{2,1,0:T(8,128)(2,1)}, u32[]{:S(2)}) copy-start(bf16[2,192,576]{2,1,0:T(8,128)(2,1)} %param.10) | copy-start | bytes 1327108
  4.8 1.2 copy-start.4
  6.0 18.8 %copy-start.1 = (bf16[2,768,192]{1,2,0:T(8,128)(2,1)S(1)}, bf16[2,768,192]{1,2,0:T(8,128)(2,1)}, u32[]{:S(2)}) copy-start(bf16[2,768,192]{1,2,0:T(8,128)(2,1)} %param.15) | copy-start | bytes 1769476
  6.7 18.1 %copy-start.2 = (bf16[2,192,768]{2,1,0:T(8,128)(2,1)S(1)}, bf16[2,192,768]{2,1,0:T(8,128)(2,1)}, u32[]{:S(2)}) copy-start(bf16[2,192,768]{2,1,0:T(8,128)(2,1)} %param.14) | copy-start | bytes 1769476
  18.4 7.3 %copy-start.5 = (f32[2,49,192]{2,0,1:T(2,128)S(1)}, f32[2,49,192]{2,0,1:T(2,128)}, u32[]{:S(2)}) copy-start(f32[2,49,192]{2,0,1:T(2,128)} %param.13) | copy-start | bytes 225796
  19.4 6.5 %copy-start = (bf16[32,64,192]{2,1,0:T(8,128)(2,1)S(1)}, bf16[32,64,192]{2,1,0:T(8,128)(2,1)}, u32[]{:S(2)}) copy-start(bf16[32,64,192]{2,1,0:T(8,128)(2,1)} %get-tuple-element.11) | copy-start | bytes 2359300
  19.4 6.4 %collective-permute-start = (bf16[3,64,192]{2,1,0:T(8,128)(2,1)S(1)}, bf16[3,64,192]{2,1,0:T(8,128)(2,1)S(1)}, u32[]{:S(2)}, u32[]{:S(2)}) collective-permute-start(bf16[3,64,192]{2,1,0:T(8,128)(2,1)S(1)} %get-tuple-element.24), channel_id=1, source_target_pairs={{0,8},{8,16},{16,24},{1,9},{9,17},{17,25},{2,10},{10,18},{18,26},{... | collective-permute-start | bytes 221192 | tf_op jit(solution)/shard_map/ppermute | solution.py:33
  23.5 5.4 %collective-permute-start.1 = (bf16[3,64,192]{2,1,0:T(8,128)(2,1)S(1)}, bf16[3,64,192]{2,1,0:T(8,128)(2,1)S(1)}, u32[]{:S(2)}, u32[]{:S(2)}) collective-permute-start(bf16[3,64,192]{2,1,0:T(8,128)(2,1)S(1)} %get-tuple-element.23), channel_id=1, source_target_pairs={{8,0},{16,8},{24,16},{9,1},{17,9},{25,17},{10,2},{18,10},{26,18},{... | collective-permute-start | bytes 221192 | tf_op jit(solution)/shard_map/ppermute | solution.py:35
  25.8 10.2 %copy-start.6 = (f32[3,1,192]{2,1,0:T(1,128)S(1)}, f32[3,1,192]{2,1,0:T(1,128)}, u32[]{:S(2)}) copy-start(f32[3,1,192]{2,1,0:T(1,128)} %get-tuple-element.38.gain_ref) | copy-start | bytes 6916
  28.9 9.3 %collective-permute-start.2 = (bf16[38,3,192]{2,1,0:T(4,128)(2,1)S(1)}, bf16[38,3,192]{2,1,0:T(4,128)(2,1)S(1)}, u32[]{:S(2)}, u32[]{:S(2)}) collective-permute-start(bf16[38,3,192]{2,1,0:T(4,128)(2,1)S(1)} %get-tuple-element.19), channel_id=1, source_target_pairs={{0,1},{1,2},{2,3},{3,4},{4,5},{5,6},{6,7},{8,9},{9,10},{10,11},{11... | collective-permute-start | bytes 131336 | tf_op jit(solution)/shard_map/ppermute | solution.py:33
  34.1 5.7 %collective-permute-start.3 = (bf16[38,3,192]{2,1,0:T(4,128)(2,1)S(1)}, bf16[38,3,192]{2,1,0:T(4,128)(2,1)S(1)}, u32[]{:S(2)}, u32[]{:S(2)}) collective-permute-start(bf16[38,3,192]{2,1,0:T(4,128)(2,1)S(1)} %get-tuple-element.20), channel_id=1, source_target_pairs={{1,0},{2,1},{3,2},{4,3},{5,4},{6,5},{7,6},{9,8},{10,9},{11,10},{12... | collective-permute-start | bytes 131336 | tf_op jit(solution)/shard_map/ppermute | solution.py:35
  69.4 31.6 %all-to-all-start = ((bf16[32,2,4,1,8,192]{5,4,2,1,3,0:T(8,128)(2,1)}), bf16[32,2,4,1,8,192]{5,4,2,1,3,0:T(8,128)(2,1)S(1)}, u32[]{:S(2)}, u32[]{:S(2)}) async-start(bf16[32,2,4,1,8,192]{5,4,2,1,3,0:T(8,128)(2,1)} %bitcast.14), calls=%async_computation | async-start | bytes 2097152 | tf_op jit(solution)/shard_map/all_to_all | solution.py:172
  149.5 5.1 %collective-permute-start.4 = (bf16[3,64,192]{2,1,0:T(8,128)(2,1)S(1)}, bf16[3,64,192]{2,1,0:T(8,128)(2,1)S(1)}, u32[]{:S(2)}, u32[]{:S(2)}) collective-permute-start(bf16[3,64,192]{2,1,0:T(8,128)(2,1)S(1)} %get-tuple-element.22), channel_id=1, source_target_pairs={{0,8},{8,16},{16,24},{1,9},{9,17},{17,25},{2,10},{10,18},{18,26},{... | collective-permute-start | bytes 221192 | tf_op jit(solution)/shard_map/ppermute | solution.py:33
  152.3 6.4 %collective-permute-start.5 = (bf16[3,64,192]{2,1,0:T(8,128)(2,1)S(1)}, bf16[3,64,192]{2,1,0:T(8,128)(2,1)S(1)}, u32[]{:S(2)}, u32[]{:S(2)}) collective-permute-start(bf16[3,64,192]{2,1,0:T(8,128)(2,1)S(1)} %get-tuple-element.21), channel_id=1, source_target_pairs={{8,0},{16,8},{24,16},{9,1},{17,9},{25,17},{10,2},{18,10},{26,18},{... | collective-permute-start | bytes 221192 | tf_op jit(solution)/shard_map/ppermute | solution.py:35
  158.8 5.9 %collective-permute-start.6 = (bf16[38,3,192]{2,1,0:T(4,128)(2,1)S(1)}, bf16[38,3,192]{2,1,0:T(4,128)(2,1)S(1)}, u32[]{:S(2)}, u32[]{:S(2)}) collective-permute-start(bf16[38,3,192]{2,1,0:T(4,128)(2,1)S(1)} %get-tuple-element.17), channel_id=1, source_target_pairs={{0,1},{1,2},{2,3},{3,4},{4,5},{5,6},{6,7},{8,9},{9,10},{10,11},{11... | collective-permute-start | bytes 131336 | tf_op jit(solution)/shard_map/ppermute | solution.py:33
  160.8 5.7 %collective-permute-start.7 = (bf16[38,3,192]{2,1,0:T(4,128)(2,1)S(1)}, bf16[38,3,192]{2,1,0:T(4,128)(2,1)S(1)}, u32[]{:S(2)}, u32[]{:S(2)}) collective-permute-start(bf16[38,3,192]{2,1,0:T(4,128)(2,1)S(1)} %get-tuple-element.18), channel_id=1, source_target_pairs={{1,0},{2,1},{3,2},{4,3},{5,4},{6,5},{7,6},{9,8},{10,9},{11,10},{12... | collective-permute-start | bytes 131336 | tf_op jit(solution)/shard_map/ppermute | solution.py:35
where the time goes:
time: 194 us; the launch traced here: 193 us
  Pallas kernels  76.2 us (39%)
  waiting for transfers between devices  34.1 us (18%)
  blocking collectives  29.6 us (15%)
  starting transfers between devices  25.6 us (13%)
  local copies, waits for them, and re-layouts  19.1 us (10%)
  other arithmetic  4.22 us (2%)
  matrix products  3.99 us (2%)
    pallas_call x2, Pallas kernels, on_device(): pl.pallas_call(conv_mlp_kernel, out_shape=(shape16,) if last else (shape1...  50.1 us
    all_to_all x1, blocking collectives, shuffled(): lax.all_to_all(result, ('row', 'col'), split_axis=0, concat_axis=0, tiled...  29.6 us
    all_to_all x1, waiting for transfers between devices, shuffled(): lax.all_to_all(outgoing, ('row', 'col'), split_axis=0, concat_axis=0, til...  24 us
    ppermute x4, starting transfers between devices, padded_2(): lax.ppermute(tail, axis, [(i, (i + 1) % count) for i in range(ends)])  14 us
    pallas_call x1, Pallas kernels, on_device(): pl.pallas_call(regular_kernel, out_shape=(shape32, shape16), grid=(height...  11.7 us
    pallas_call x1, Pallas kernels, shuffled(): pl.pallas_call(shuffle_kernel, out_shape=jax.ShapeDtypeStruct(grid.shape,...  10.3 us
    ppermute x4, waiting for transfers between devices, padded_2(): lax.ppermute(head, axis, [((i + 1) % count, i) for i in range(ends)])  9.14 us
    ppermute x4, starting transfers between devices, padded_2(): lax.ppermute(head, axis, [((i + 1) % count, i) for i in range(ends)])  6.91 us
  transfers between devices with their start and end apart: 9, of which 6 were waited for; matrix products, arithmetic and copies ran while one was open for 5% of the time, Pallas kernels for 0%

commit v1 on v0

v1 whole, which is shorter than its diff:
```python
import functools

import jax
import jax.numpy as jnp
from jax import lax
from jax.experimental import pallas as pl
from jax.experimental.pallas import tpu as pltpu
from jax.sharding import PartitionSpec as P

D = 192
HEADS = 6
WS = 8
KS = 7
LAYERS = 2
HEAD = 32
AREA = WS * WS
HALO = KS // 2

epsilon = 1e-05
LOG2E = 1.4426950408889634
VALUE_SCALE = 2.0**-8
EXP_CAP = 3.3895313892515355e38
MESH = pl.DeviceIdType.MESH
SIDES = [(d, a) for d in (-1, 0, 1) for a in (-1, 0, 1) if d or a]


def norm(values, gain):
    centre = jnp.mean(values, axis=-1, keepdims=True)
    centred = values - centre
    spread = jnp.mean(centred * centred, axis=-1, keepdims=True)
    return centred * lax.rsqrt(spread + epsilon) * gain


def score_bias(lookup_table):
    places = jnp.arange(AREA, dtype=jnp.int32)
    row, col = places // WS, places % WS
    offsets = (row[:, None] - row[None, :] + WS - 1) * (2 * WS - 1) + (
        col[:, None] - col[None, :] + WS - 1
    )
    entries = jnp.arange((2 * WS - 1) * (2 * WS - 1), dtype=jnp.int32)
    selector = (offsets.reshape(-1)[:, None] == entries[None, :]).astype(jnp.float32)
    expanded = jnp.dot(lookup_table, selector.T, precision=lax.Precision.HIGHEST) * LOG2E
    return expanded.reshape(HEADS, AREA, AREA).transpose(1, 0, 2).reshape(AREA, HEADS * AREA)


def attention(normed, qkv_ref, proj_ref, bias_ref):
    count = normed.shape[0] // AREA
    query, key, value = (
        jnp.dot(normed, qkv_ref[part], preferred_element_type=jnp.float32).astype(jnp.bfloat16)
        for part in range(3)
    )
    lane_head = lax.broadcasted_iota(jnp.int32, (1, D), 1) // HEAD
    masks = [(lane_head == head).astype(jnp.bfloat16) for head in range(HEADS)]
    value_masks = [mask * VALUE_SCALE for mask in masks]
    sums = jnp.concatenate([jnp.broadcast_to(mask, (AREA, D)) for mask in value_masks], axis=0)
    bias = bias_ref[...]
    outs, exps = [], []
    for window in range(count):
        rows = slice(window * AREA, (window + 1) * AREA)
        keys = jnp.concatenate([key[rows] * mask for mask in masks], axis=0)
        scores = lax.dot_general(
            query[rows], keys, (((1,), (1,)), ((), ())), preferred_element_type=jnp.float32
        )
        exped = jnp.minimum(jnp.exp2(scores * (HEAD**-0.5 * LOG2E) + bias), EXP_CAP)
        exped = exped.astype(jnp.bfloat16)
        values = jnp.concatenate([value[rows] * mask for mask in value_masks], axis=0)
        outs.append(jnp.dot(exped, values, preferred_element_type=jnp.float32))
        exps.append(exped)
    total = jnp.dot(jnp.concatenate(exps, axis=0), sums, preferred_element_type=jnp.float32)
    attended = (jnp.concatenate(outs, axis=0) / total).astype(jnp.bfloat16)
    branch = jnp.dot(attended, proj_ref[...], preferred_element_type=jnp.float32)
    return branch.astype(jnp.bfloat16).astype(jnp.float32)


def regular_kernel(x_ref, gain_ref, qkv_ref, proj_ref, bias_ref, after_ref, normed_ref):
    rows, width = x_ref.shape[0], x_ref.shape[1]
    current = x_ref[...].astype(jnp.float32)
    normed = norm(current.reshape(rows * width, D), gain_ref[0])
    windows = normed.reshape(WS, width // WS, WS, D).transpose(1, 0, 2, 3).reshape(rows * width, D)
    branch = attention(windows.astype(jnp.bfloat16), qkv_ref, proj_ref, bias_ref)
    branch = branch.reshape(width // WS, WS, WS, D).transpose(1, 0, 2, 3).reshape(rows, width, D)
    after = current + branch
    after_ref[...] = after
    normed_ref[...] = norm(after, gain_ref[1]).astype(jnp.bfloat16)


def greet(everyone):
    rows, cols = lax.axis_size("row"), lax.axis_size("col")
    my_row, my_col = lax.axis_index("row"), lax.axis_index("col")
    barrier = pltpu.get_barrier_semaphore()
    if everyone:

        @pl.loop(0, rows * cols)
        def _(device):
            row, col = device // cols, device % cols

            @pl.when((row != my_row) | (col != my_col))
            def _():
                pl.semaphore_signal(barrier, 1, device_id=(row, col), device_id_type=MESH)

        pl.semaphore_wait(barrier, rows * cols - 1)
    else:
        for down, across in SIDES:
            row, col = my_row + down, my_col + across
            inside = (row >= 0) & (row < rows) & (col >= 0) & (col < cols)

            @pl.when(inside)
            def _():
                pl.semaphore_signal(barrier, 1, device_id=(row, col), device_id_type=MESH)

        beside_rows = (my_row > 0).astype(jnp.int32) + (my_row < rows - 1).astype(jnp.int32)
        beside_cols = (my_col > 0).astype(jnp.int32) + (my_col < cols - 1).astype(jnp.int32)
        pl.semaphore_wait(barrier, (1 + beside_rows) * (1 + beside_cols) - 1)


def exchange(normed_ref, wide, beside, above, corner, send_sem, recv_sem):
    rows, cols = lax.axis_size("row"), lax.axis_size("col")
    my_row, my_col = lax.axis_index("row"), lax.axis_index("col")
    height, blocks = normed_ref.shape[0], normed_ref.shape[1]
    width = blocks * 8
    links = []
    for number, (down, across) in enumerate(SIDES):
        row, col = my_row + down, my_col + across
        there = (row >= 0) & (row < rows) & (col >= 0) & (col < cols)
        back_row, back_col = my_row - down, my_col - across
        here = (back_row >= 0) & (back_row < rows) & (back_col >= 0) & (back_col < cols)
        picked = {-1: slice(0, HALO), 0: slice(0, height), 1: slice(height - HALO, height)}[down]
        if across == 0:
            source, target = normed_ref.at[picked], above.at[(1 - down) // 2]
        else:
            block = 0 if across < 0 else blocks - 1
            source = normed_ref.at[picked, block]
            side = (1 - across) // 2
            target = beside.at[side] if down == 0 else corner.at[(1 - down) // 2, side]
        copy = pltpu.make_async_remote_copy(
            source,
            target,
            send_sem.at[number],
            recv_sem.at[number],
            device_id=(row, col),
            device_id_type=MESH,
        )
        links.append((down, across, there, here, copy))
        pl.when(there)(copy.start)

    @pl.loop(0, height)
    def _(r):
        wide[HALO + r, 8 : 8 + width, :] = normed_ref[r].astype(jnp.float32).reshape(width, D)

    for down, across, there, here, copy in links:
        rows_at = {1: slice(0, HALO), 0: slice(HALO, HALO + height), -1: slice(HALO + height, None)}
        cols_at = {1: slice(0, 8), 0: slice(8, 8 + width), -1: slice(8 + width, None)}
        at = (rows_at[down], cols_at[across])

        @pl.when(here)
        def _():
            copy.wait_recv()
            if across == 0:
                landed = above[(1 - down) // 2].astype(jnp.float32).reshape(HALO, width, D)
            elif down == 0:
                landed = beside[(1 - across) // 2].astype(jnp.float32)
            else:
                landed = corner[(1 - down) // 2, (1 - across) // 2].astype(jnp.float32)
            wide[at[0], at[1], :] = landed

        @pl.when(jnp.logical_not(here))
        def _():
            wide[at[0], at[1], :] = jnp.zeros_like(wide[at[0], at[1], :])

        pl.when(there)(copy.wait_send)


def mix(base, after, wide, taps, conv, gain_ref, up_ref, down_ref):
    rows, width = after.shape[0], after.shape[1]

    for left in range(0, width, 8):
        for lanes in (slice(0, 128), slice(128, D)):
            sums = after[:, left : left + 8, lanes]
            for v in range(KS):
                start = left + 8 - HALO + v
                cells = wide[pl.ds(base, rows + KS - 1), start : start + 8, lanes]
                for u in range(KS):
                    sums = sums + cells[u : u + rows] * taps[u * KS + v, :, lanes][None]
            conv[:, left : left + 8, lanes] = sums

    flat = conv[...].reshape(rows * width, D)
    normed = norm(flat, gain_ref[2]).astype(jnp.bfloat16)
    up = jnp.dot(normed, up_ref[...], preferred_element_type=jnp.float32)
    hidden = (0.5 * up * (1.0 + lax.erf(up * 0.5**0.5))).astype(jnp.bfloat16)
    outcome = flat + jnp.dot(hidden, down_ref[...], preferred_element_type=jnp.float32)
    return outcome.astype(jnp.bfloat16)


def first_mix_kernel(
    normed_ref,
    after_ref,
    gain_ref,
    taps_ref,
    up_ref,
    down_ref,
    out_ref,
    received,
    wide,
    taps,
    conv,
    beside,
    above,
    corner,
    halo_send,
    halo_recv,
    outgoing,
    send_sem,
    recv_sem,
):
    rows, width = after_ref.shape[0], after_ref.shape[1]
    row_count, col_count, row_repeat, pairs, col_piece = received.shape[:5]
    per_step = rows // (2 * pairs)
    my_row, my_col = lax.axis_index("row"), lax.axis_index("col")
    step = pl.program_id(0)

    @pl.when(step == 0)
    def _():
        greet(True)
        taps[...] = jnp.broadcast_to(taps_ref[...][:, None, :], taps.shape)
        exchange(normed_ref, wide, beside, above, corner, halo_send, halo_recv)

    current = mix(step * rows, after_ref, wide, taps, conv, gain_ref, up_ref, down_ref)
    out_ref[...] = current.reshape(rows, width, D)
    following = norm(current.astype(jnp.float32), gain_ref[3]).reshape(rows, width, D)

    for k in range(per_step):
        for pair in range(pairs):
            row = (k * pairs + pair) * 2
            packed = jnp.concatenate([following[row], following[row + 1]], axis=-1)
            for col in range(col_count):
                piece = packed[col * col_piece : (col + 1) * col_piece]
                outgoing[step * per_step + k, col, pair] = piece.astype(jnp.bfloat16)

    def remote(chunk, col):
        return pltpu.make_async_remote_copy(
            outgoing.at[chunk, col],
            received.at[my_row, my_col, chunk // row_count],
            send_sem.at[chunk, col],
            recv_sem.at[my_row, my_col, chunk // row_count],
            device_id=(chunk % row_count, col),
            device_id_type=MESH,
        )

    for k in range(per_step):
        chunk = step * per_step + k

        @pl.loop(0, col_count)
        def _(turn):
            col = (my_col + turn) % col_count
            mine = (chunk % row_count == my_row) & (col == my_col)

            @pl.when(mine)
            def _():
                pltpu.make_async_copy(
                    outgoing.at[chunk, col],
                    received.at[my_row, my_col, chunk // row_count],
                    recv_sem.at[my_row, my_col, chunk // row_count],
                ).start()

            @pl.when(jnp.logical_not(mine))
            def _():
                remote(chunk, col).start()

    @pl.when(step == pl.num_programs(0) - 1)
    def _():
        @pl.loop(0, row_count * row_repeat)
        def _(chunk):
            @pl.loop(0, col_count)
            def _(col):
                mine = (chunk % row_count == my_row) & (col == my_col)

                @pl.when(jnp.logical_not(mine))
                def _():
                    remote(chunk, col).wait_send()

                row, repeat = chunk % row_count, chunk // row_count
                pltpu.make_async_copy(
                    outgoing.at[chunk, col],
                    received.at[row, col, repeat],
                    recv_sem.at[row, col, repeat],
                ).wait()


def shuffle_kernel(
    x_ref, qkv_ref, proj_ref, bias_ref, returned, outgoing, send_sem, recv_sem
):
    row_count, col_count, row_repeat, pairs, col_piece = returned.shape[:5]
    per_b = col_count // WS
    across = per_b * col_piece
    my_row, my_col = lax.axis_index("row"), lax.axis_index("col")
    step = pl.program_id(0)

    @pl.when(step == 0)
    def _():
        greet(True)

    tokens = x_ref[:, :, :, 0].astype(jnp.float32).transpose(0, 2, 1, 3, 4)
    tokens = tokens.reshape(WS, WS, per_b, col_piece, 2 * D)
    if per_b == 1:
        tokens = tokens[:, :, 0]
    else:
        tokens = jnp.concatenate([tokens[:, :, part] for part in range(per_b)], axis=2)
    results = []
    for half in range(2):
        windows = jnp.swapaxes(tokens[..., half * D : (half + 1) * D], 1, 2)
        windows = windows.transpose(1, 0, 2, 3).reshape(across * AREA, D)
        branch = attention(windows.astype(jnp.bfloat16), qkv_ref, proj_ref, bias_ref)
        branch = branch.reshape(across, WS, WS, D).transpose(1, 0, 2, 3)
        results.append(jnp.swapaxes(branch, 1, 2))
    packed = jnp.concatenate(results, axis=-1).reshape(row_count, row_repeat, WS, across, 2 * D)
    for col in range(col_count):
        part = col % per_b
        piece = packed[:, :, col // per_b, part * col_piece : (part + 1) * col_piece]
        outgoing[step, :, col] = piece.astype(jnp.bfloat16)

    def remote(pair, row, col):
        return pltpu.make_async_remote_copy(
            outgoing.at[pair, row, col],
            returned.at[my_row, my_col, :, pair],
            send_sem.at[pair, row, col],
            recv_sem.at[pair, my_row, my_col],
            device_id=(row, col),
            device_id_type=MESH,
        )

    def local(pair, row, col):
        return pltpu.make_async_copy(
            outgoing.at[pair, row, col],
            returned.at[row, col, :, pair],
            recv_sem.at[pair, row, col],
        )

    @pl.loop(0, row_count)
    def _(row):
        @pl.loop(0, col_count)
        def _(turn):
            col = (my_col + turn) % col_count
            mine = (row == my_row) & (col == my_col)
            pl.when(mine)(lambda: local(step, row, col).start())
            pl.when(jnp.logical_not(mine))(lambda: remote(step, row, col).start())

    @pl.when(step == pl.num_programs(0) - 1)
    def _():
        @pl.loop(0, row_count * pairs)
        def _(both):
            pair, row = both // row_count, both % row_count

            @pl.loop(0, col_count)
            def _(col):
                mine = (row == my_row) & (col == my_col)
                pl.when(jnp.logical_not(mine))(lambda: remote(pair, row, col).wait_send())
                local(pair, row, col).wait()


def last_mix_kernel(
    current_ref,
    returned_ref,
    gain_ref,
    taps_ref,
    up_ref,
    down_ref,
    out_ref,
    after,
    normed,
    wide,
    taps,
    conv,
    beside,
    above,
    corner,
    halo_send,
    halo_recv,
):
    rows, width = out_ref.shape[0], out_ref.shape[1]
    row_count, col_count, row_repeat, pairs, col_piece = returned_ref.shape[:5]
    step = pl.program_id(0)

    @pl.when(step == 0)
    def _():
        taps[...] = jnp.broadcast_to(taps_ref[...][:, None, :], taps.shape)

        @pl.loop(0, row_count * row_repeat)
        def _(chunk):
            for pair in range(pairs):
                packed = returned_ref[chunk % row_count, :, chunk // row_count, pair]
                packed = packed.astype(jnp.float32).reshape(width, 2 * D)
                for half in range(2):
                    row = (chunk * pairs + pair) * 2 + half
                    total = current_ref[row].astype(jnp.float32)
                    total = total + packed[:, half * D : (half + 1) * D]
                    after[row] = total
                    normed[row] = (
                        norm(total, gain_ref[1]).reshape(width // 8, 8, D).astype(jnp.bfloat16)
                    )

        greet(False)
        exchange(normed, wide, beside, above, corner, halo_send, halo_recv)

    base = step * rows
    current = mix(
        base, after.at[pl.ds(base, rows)], wide, taps, conv, gain_ref, up_ref, down_ref
    )
    out_ref[...] = current.reshape(rows, width, D)


def whole(shape):
    return pl.BlockSpec(shape, lambda i: (0,) * len(shape))


def stripe(width):
    return pl.BlockSpec((WS, width, D), lambda i: (i, 0, 0))


def mix_scratch(height, width):
    dma = pltpu.SemaphoreType.DMA
    return [
        pltpu.VMEM((height + 2 * HALO, width + 16, D), jnp.float32),
        pltpu.VMEM((KS * KS, 8, D), jnp.float32),
        pltpu.VMEM((WS, width, D), jnp.float32),
        pltpu.VMEM((2, height, 8, D), jnp.bfloat16),
        pltpu.VMEM((2, HALO, width // 8, 8, D), jnp.bfloat16),
        pltpu.VMEM((2, 2, HALO, 8, D), jnp.bfloat16),
        dma((len(SIDES),)),
        dma((len(SIDES),)),
    ]


def on_device(
    tokens, norm_gain, qkv_weight, proj_weight, bias_table, conv_weight, up_weight, down_weight
):
    height, width = tokens.shape[0], tokens.shape[1]
    row_count, col_count = lax.axis_size("row"), lax.axis_size("col")
    row_repeat = max(1, WS // row_count)
    row_piece = height // row_repeat // row_count
    col_piece = width // col_count
    pairs = row_piece // 2
    dma = pltpu.SemaphoreType.DMA
    shape32 = jax.ShapeDtypeStruct(tokens.shape, jnp.float32)
    shape16 = jax.ShapeDtypeStruct(tokens.shape, jnp.bfloat16)
    blocked = (height, width // 8, 8, D)
    moved = jax.ShapeDtypeStruct(
        (row_count, col_count, row_repeat, pairs, col_piece, 2 * D), jnp.bfloat16
    )
    qkv_parts = qkv_weight.reshape(LAYERS, D, 3, D).transpose(0, 2, 1, 3)
    biases = [score_bias(bias_table[layer]) for layer in range(LAYERS)]
    gains = jnp.concatenate([norm_gain, jnp.roll(norm_gain[:, :1], -1, axis=0)], axis=1)
    gains = gains[:, :, None, :]
    gain_shape = gains.shape[1:]
    weight_specs = [
        whole(gain_shape),
        whole((KS * KS, D)),
        whole(up_weight.shape[1:]),
        whole(down_weight.shape[1:]),
    ]
    attention_specs = [whole(qkv_parts.shape[1:]), whole((D, D)), whole(biases[0].shape)]

    after, normed_two = pl.pallas_call(
        regular_kernel,
        out_shape=(shape32, shape16),
        grid=(height // WS,),
        in_specs=[stripe(width), whole(gain_shape)] + attention_specs,
        out_specs=(stripe(width), stripe(width)),
        name="regular_attention",
    )(tokens, gains[0], qkv_parts[0], proj_weight[0], biases[0])

    current, received = pl.pallas_call(
        first_mix_kernel,
        out_shape=(shape16, moved),
        grid=(height // WS,),
        in_specs=[whole(blocked), stripe(width)] + weight_specs,
        out_specs=(stripe(width), pl.BlockSpec(memory_space=pl.ANY)),
        scratch_shapes=mix_scratch(height, width)
        + [
            pltpu.VMEM(
                (row_repeat * row_count, col_count, pairs, col_piece, 2 * D), jnp.bfloat16
            ),
            dma((row_repeat * row_count, col_count)),
            dma((row_count, col_count, row_repeat)),
        ],
        compiler_params=pltpu.CompilerParams(collective_id=0, has_side_effects=True),
        name="first_mix",
    )(
        normed_two.reshape(blocked),
        after,
        gains[0],
        conv_weight[0],
        up_weight[0],
        down_weight[0],
    )

    returned = pl.pallas_call(
        shuffle_kernel,
        out_shape=moved,
        grid=(pairs,),
        in_specs=[
            pl.BlockSpec(
                (row_count, col_count, row_repeat, 1, col_piece, 2 * D),
                lambda i: (0, 0, 0, i, 0, 0),
            )
        ]
        + attention_specs,
        out_specs=pl.BlockSpec(memory_space=pl.ANY),
        scratch_shapes=[
            pltpu.VMEM(
                (pairs, row_count, col_count, row_repeat, col_piece, 2 * D), jnp.bfloat16
            ),
            dma((pairs, row_count, col_count)),
            dma((pairs, row_count, col_count)),
        ],
        compiler_params=pltpu.CompilerParams(collective_id=1, has_side_effects=True),
        name="shuffle_attention",
    )(received, qkv_parts[1], proj_weight[1], biases[1])

    return pl.pallas_call(
        last_mix_kernel,
        out_shape=shape16,
        grid=(height // WS,),
        in_specs=[whole(tokens.shape), whole(moved.shape)] + weight_specs,
        out_specs=stripe(width),
        scratch_shapes=[
            pltpu.VMEM(tokens.shape, jnp.float32),
            pltpu.VMEM(blocked, jnp.bfloat16),
        ]
        + mix_scratch(height, width),
        compiler_params=pltpu.CompilerParams(collective_id=2, has_side_effects=True),
        name="last_mix",
    )(current, returned, gains[1], conv_weight[1], up_weight[1], down_weight[1])


def solution(mesh):
    in_specs = (P("row", "col", None), P(), P(), P(), P(), P(), P(), P())
    return jax.shard_map(
        on_device, mesh=mesh, in_specs=in_specs, out_specs=P("row", "col", None), check_vma=False
    )
```

time: 194 us -> 139 us (0.72)
  Pallas kernels: 76.2 us -> 122 us
  waiting for transfers between devices: 34.1 us -> 0 us
  blocking collectives: 29.6 us -> 0 us
  starting transfers between devices: 25.6 us -> 0 us
  local copies, waits for them, and re-layouts: 19.1 us -> 11.3 us
  other arithmetic: 4.22 us -> 0.1 us
    pallas_call x4 -> x3, Pallas kernels: 64.5 us -> 110 us  [the longest x1 43.1 us: on_device(): pl.pallas_call(first_mix_kernel, out_shape=(shape16, moved), grid=(height...]
    all_to_all x1 -> x0, blocking collectives: 29.6 us -> none  [shuffled(): lax.all_to_all(result, ('row', 'col'), split_axis=0, concat_axis=0, tiled...]
    all_to_all x1 -> x0, waiting for transfers between devices: 24 us -> none  [shuffled(): lax.all_to_all(outgoing, ('row', 'col'), split_axis=0, concat_axis=0, til...]
    ppermute x8 -> x0, starting transfers between devices: 20.9 us -> none  [the longest x4 14 us: padded_2(): lax.ppermute(tail, axis, [(i, (i + 1) % count) for i in range(ends)])]
    ppermute x8 -> x0, waiting for transfers between devices: 10.1 us -> none  [the longest x4 9.14 us: padded_2(): lax.ppermute(head, axis, [((i + 1) % count, i) for i in range(ends)])]
    all_to_all x1 -> x0, starting transfers between devices: 4.65 us -> none  [shuffled(): lax.all_to_all(outgoing, ('row', 'col'), split_axis=0, concat_axis=0, til...]
    concatenate x3 -> x1, other arithmetic: 4.13 us -> 0.01 us  [on_device(): jnp.concatenate([norm_gain, jnp.roll(norm_gain[:, :1], -1, axis=0)], axis=1)]
    reshape x2 -> x0, local copies, waits for them, and re-layouts: 3.7 us -> none  [the longest x1 2.35 us: shuffled(): normed.reshape(row_repeat, row_count, row_piece, col_repeat, col_count, c...]
  transfers between devices with their start and end apart: 9 -> 0, of which waited for: 6 -> 0; matrix products, arithmetic and copies ran while one was open for 5% -> 0% of each run, Pallas kernels for 0% -> 0%
where the time goes in v1:
time: 139 us; the launch traced here: 137 us
  Pallas kernels  122 us (88%)
  local copies, waits for them, and re-layouts  11.3 us (8%)
  matrix products  3.99 us (3%)
    pallas_call x1, Pallas kernels, on_device(): pl.pallas_call(first_mix_kernel, out_shape=(shape16, moved), grid=(height...  43.1 us
    pallas_call x1, Pallas kernels, on_device(): pl.pallas_call(last_mix_kernel, out_shape=shape16, grid=(height // WS,),...  36.4 us
    pallas_call x1, Pallas kernels, on_device(): pl.pallas_call(shuffle_kernel, out_shape=moved, grid=(pairs,), in_specs=[...  30.8 us
    pallas_call x1, Pallas kernels, on_device(): pl.pallas_call(regular_kernel, out_shape=(shape32, shape16), grid=(height...  11.6 us
    unnamed x16, local copies, waits for them, and re-layouts  4.41 us
    dot_general x2, matrix products, score_bias(): jnp.dot(lookup_table, selector.T, precision=lax.Precision.HIGHEST) * LOG2E  3.99 us

profile of v1, /device:TPU:1, one launch (start us, length us, event | category | flops | bytes accessed | tf_op | source)
XLA Modules:
  0.0 137.4 jit_solution(3308083039448393226)
XLA Ops:
  0.0 0.0 copy-start.5
  0.0 0.0 copy-start.2
  0.0 0.1 add_add_fusion
  0.1 0.1 add.66
  0.2 0.8 fusion.6
  1.0 2.0 %fusion.1 = f32[6,4096]{1,0:T(8,128)S(1)} fusion(s32[4096]{0:T(1024)S(1)} %add.66, f32[1,6,225]{2,0,1:T(1,128)S(1)} %get-tuple-element.24), kind=kOutput, calls=%fused_computation.3 | convolution fusion | flops 67301376 | bytes 120088 | tf_op jit(solution)/shard_map/dot_general | solution.py:42
  3.0 0.1 reshape.106
  3.1 0.0 copy-start.3
  3.1 0.1 copy.40
  3.2 0.7 reshape.107.bias_ref
  3.9 0.0 copy-done.5
  4.0 0.6 slice_bitcast_fusion.6
  4.6 0.0 copy-done.2
  4.6 0.2 copy.15
  4.8 0.0 copy-start.4
  4.8 0.0 copy-start
  4.8 0.3 copy.16
  5.1 0.9 slice_bitcast_fusion
  6.0 0.0 copy-done.3
  6.0 0.0 copy-start.1
  6.0 0.7 slice_bitcast_fusion.4
  6.7 11.6 %regular_attention.1 = (f32[32,64,192]{2,1,0:T(8,128)}, bf16[32,64,192]{2,1,0:T(8,128)(2,1)}) custom-call(bf16[32,64,192]{2,1,0:T(8,128)(2,1)} %x_ref.1, f32[4,1,192]{2,1,0:T(1,128)} %get-tuple-element.26.gain_ref, bf16[3,192,192]{2,1,0:T(8,128)(2,1)} %get-tuple-element.18.qkv_ref, bf16[192,192]{1,0:T(8,128)(2,1)} %get-tuple-element.20.proj_ref, ...), custom_call_target="tpu_custom_call" | custom-call | tf_op jit(solution)/shard_map/regular_attention/pallas_call | solution.py:462
  18.3 0.0 copy-done.4
  18.3 0.1 fusion.5
  18.4 0.7 copy_bitcast_fusion.2
  19.0 0.0 copy-done
  19.1 0.9 copy.27
  20.0 0.0 copy-done.1
  20.0 0.9 slice_bitcast_fusion.2
  20.9 43.1 %first_mix.1 = (bf16[32,64,192]{2,1,0:T(8,128)(2,1)}, bf16[4,8,2,2,8,384]{5,4,3,2,1,0:T(8,128)(2,1)}) custom-call(bf16[32,8,8,192]{3,2,1,0:T(8,128)(2,1)} %bitcast.45, f32[32,64,192]{2,1,0:T(8,128)} %get-tuple-element.10.after_ref, f32[4,1,192]{2,1,0:T(1,128)} %get-tuple-element.26.gain_ref, f32[49,192]{1,0:T(8,128)} %get-tuple-element.32.taps_ref, ...), custom_call_target="tpu_custom_call" | custom-call | tf_op jit(solution)/shard_map/first_mix/pallas_call | solution.py:471
  64.0 2.0 %fusion = f32[6,4096]{1,0:T(8,128)S(1)} fusion(s32[4096]{0:T(1024)S(1)} %add.66, f32[1,6,225]{2,0,1:T(1,128)S(1)} %get-tuple-element.23), kind=kOutput, calls=%fused_computation.1 | convolution fusion | flops 67301376 | bytes 120088 | tf_op jit(solution)/shard_map/dot_general | solution.py:42
  66.0 0.1 reshape.109
  66.1 0.1 copy.39
  66.2 0.7 reshape.110.bias_ref
  66.9 30.8 %shuffle_attention.1.returned_ref = bf16[4,8,2,2,8,384]{5,4,3,2,1,0:T(8,128)(2,1)} custom-call(bf16[4,8,2,2,8,384]{5,4,3,2,1,0:T(8,128)(2,1)} %get-tuple-element.12.x_ref, bf16[3,192,192]{2,1,0:T(8,128)(2,1)} %get-tuple-element.17.qkv_ref, bf16[192,192]{1,0:T(8,128)(2,1)} %get-tuple-element.19.proj_ref, f32[64,384]{1,0:T(8,128)} %reshape.110.bias_ref), custom_call_target="tpu_custom_call" | custom-call | tf_op jit(solution)/shard_map/shuffle_attention/pallas_call | solution.py:496
  97.8 0.9 copy.30
  98.7 36.4 %last_mix.1 = bf16[32,64,192]{2,1,0:T(8,128)(2,1)} custom-call(bf16[32,64,192]{2,1,0:T(8,128)(2,1)} %get-tuple-element.11.current_ref, bf16[4,8,2,2,8,384]{5,4,3,2,1,0:T(8,128)(2,1)} %shuffle_attention.1.returned_ref, f32[4,1,192]{2,1,0:T(1,128)} %get-tuple-element.25.gain_ref, f32[49,192]{1,0:T(8,128)} %get-tuple-element.31.taps_ref, ...), custom_call_target="tpu_custom_call" | custom-call | tf_op jit(solution)/shard_map/last_mix/pallas_call | solution.py:519
  135.1 2.3 %copy.42 = bf16[32,64,192]{2,1,0:T(8,128)(2,1)} copy(bf16[32,64,192]{2,1,0:T(8,128)(2,1)} %last_mix.1) | data formatting | bytes 1572864
  (4 shorter events, 0.1 us)
Async XLA Ops:
  0.0 3.9 %copy-start.5 = (f32[2,3,192]{2,0,1:T(2,128)S(1)}, f32[2,3,192]{2,0,1:T(2,128)}, u32[]{:S(2)}) copy-start(f32[2,3,192]{2,0,1:T(2,128)} %param.9) | copy-start | bytes 13828
  0.0 4.6 %copy-start.2 = (bf16[2,192,576]{2,1,0:T(8,128)(2,1)S(1)}, bf16[2,192,576]{2,1,0:T(8,128)(2,1)}, u32[]{:S(2)}) copy-start(bf16[2,192,576]{2,1,0:T(8,128)(2,1)} %param.10) | copy-start | bytes 1327108
  3.1 2.9 %copy-start.3 = (bf16[2,192,192]{2,1,0:T(8,128)(2,1)S(1)}, bf16[2,192,192]{2,1,0:T(8,128)(2,1)}, u32[]{:S(2)}) copy-start(bf16[2,192,192]{2,1,0:T(8,128)(2,1)} %param.11) | copy-start | bytes 442372
  4.8 13.5 %copy-start.4 = (f32[2,49,192]{2,0,1:T(2,128)S(1)}, f32[2,49,192]{2,0,1:T(2,128)}, u32[]{:S(2)}) copy-start(f32[2,49,192]{2,0,1:T(2,128)} %param.13) | copy-start | bytes 225796
  4.8 14.2 %copy-start = (bf16[2,768,192]{1,2,0:T(8,128)(2,1)S(1)}, bf16[2,768,192]{1,2,0:T(8,128)(2,1)}, u32[]{:S(2)}) copy-start(bf16[2,768,192]{1,2,0:T(8,128)(2,1)} %param.15) | copy-start | bytes 1769476
  6.0 14.0 %copy-start.1 = (bf16[2,192,768]{2,1,0:T(8,128)(2,1)S(1)}, bf16[2,192,768]{2,1,0:T(8,128)(2,1)}, u32[]{:S(2)}) copy-start(bf16[2,192,768]{2,1,0:T(8,128)(2,1)} %param.14) | copy-start | bytes 1769476

commit v2 on v1

--- a/solution.py
+++ b/solution.py
@@ -15,6 +15,7 @@
 HEAD = 32
 AREA = WS * WS
 HALO = KS // 2
+LANES = 128
 
 epsilon = 1e-05
 LOG2E = 1.4426950408889634
@@ -31,22 +32,26 @@
     return centred * lax.rsqrt(spread + epsilon) * gain
 
 
-def score_bias(lookup_table):
+def score_biases(lookup_tables):
     places = jnp.arange(AREA, dtype=jnp.int32)
     row, col = places // WS, places % WS
     offsets = (row[:, None] - row[None, :] + WS - 1) * (2 * WS - 1) + (
         col[:, None] - col[None, :] + WS - 1
     )
     entries = jnp.arange((2 * WS - 1) * (2 * WS - 1), dtype=jnp.int32)
-    selector = (offsets.reshape(-1)[:, None] == entries[None, :]).astype(jnp.float32)
-    expanded = jnp.dot(lookup_table, selector.T, precision=lax.Precision.HIGHEST) * LOG2E
-    return expanded.reshape(HEADS, AREA, AREA).transpose(1, 0, 2).reshape(AREA, HEADS * AREA)
+    selector = (offsets.reshape(-1)[None, :] == entries[:, None]).astype(jnp.float32)
+    tables = lookup_tables.reshape(LAYERS * HEADS, -1)
+    expanded = jnp.dot(tables, selector, precision=lax.Precision.HIGHEST) * LOG2E
+    expanded = expanded.reshape(LAYERS, HEADS, AREA, AREA).transpose(0, 2, 1, 3)
+    return expanded.reshape(LAYERS, AREA, HEADS * AREA)
 
 
 def attention(normed, qkv_ref, proj_ref, bias_ref):
     count = normed.shape[0] // AREA
     query, key, value = (
-        jnp.dot(normed, qkv_ref[part], preferred_element_type=jnp.float32).astype(jnp.bfloat16)
+        jnp.dot(
+            normed, qkv_ref[:, part * D : (part + 1) * D], preferred_element_type=jnp.float32
+        ).astype(jnp.bfloat16)
         for part in range(3)
     )
     lane_head = lax.broadcasted_iota(jnp.int32, (1, D), 1) // HEAD
@@ -75,13 +80,13 @@
 def regular_kernel(x_ref, gain_ref, qkv_ref, proj_ref, bias_ref, after_ref, normed_ref):
     rows, width = x_ref.shape[0], x_ref.shape[1]
     current = x_ref[...].astype(jnp.float32)
-    normed = norm(current.reshape(rows * width, D), gain_ref[0])
+    normed = norm(current.reshape(rows * width, D), gain_ref[0, 0:1])
     windows = normed.reshape(WS, width // WS, WS, D).transpose(1, 0, 2, 3).reshape(rows * width, D)
     branch = attention(windows.astype(jnp.bfloat16), qkv_ref, proj_ref, bias_ref)
     branch = branch.reshape(width // WS, WS, WS, D).transpose(1, 0, 2, 3).reshape(rows, width, D)
     after = current + branch
     after_ref[...] = after
-    normed_ref[...] = norm(after, gain_ref[1]).astype(jnp.bfloat16)
+    normed_ref[...] = norm(after, gain_ref[0, 1:2]).astype(jnp.bfloat16)
 
 
 def greet(everyone):
@@ -170,21 +175,47 @@
         pl.when(there)(copy.wait_send)
 
 
-def mix(base, after, wide, taps, conv, gain_ref, up_ref, down_ref):
+def shift(wide, low, high, taps, taps_ref):
+    width = low.shape[2]
+    upper = taps_ref[:, LANES:]
+    taps[0] = jnp.broadcast_to(taps_ref[:, :LANES][:, None, :], taps.shape[1:])
+    both = jnp.concatenate([upper, upper], axis=-1)
+    taps[1] = jnp.broadcast_to(both[:, None, :], taps.shape[1:])
+
+    @pl.loop(0, wide.shape[0])
+    def _(r):
+        for v in range(KS):
+            start = 8 - HALO + v
+            low[v, r] = wide[r, start : start + width, :LANES]
+            left = wide[r, start : start + width // 2, LANES:]
+            right = wide[r, start + width // 2 : start + width, LANES:]
+            high[v, r] = jnp.concatenate([left, right], axis=-1)
+
+
+def mix(base, after, low, high, taps, conv, gain, up_ref, down_ref):
     rows, width = after.shape[0], after.shape[1]
 
+    def tapped(cells, weights, left):
+        sums = None
+        for v in range(KS):
+            for u in range(KS):
+                term = cells[v, pl.ds(base + u, rows), left : left + 8, :]
+                term = term * weights[u * KS + v][None]
+                sums = term if sums is None else sums + term
+        return sums
+
     for left in range(0, width, 8):
-        for lanes in (slice(0, 128), slice(128, D)):
-            sums = after[:, left : left + 8, lanes]
-            for v in range(KS):
-                start = left + 8 - HALO + v
-                cells = wide[pl.ds(base, rows + KS - 1), start : start + 8, lanes]
-                for u in range(KS):
-                    sums = sums + cells[u : u + rows] * taps[u * KS + v, :, lanes][None]
-            conv[:, left : left + 8, lanes] = sums
+        at = slice(left, left + 8)
+        conv[:, at, :LANES] = after[:, at, :LANES] + tapped(low, taps.at[0], left)
+    for left in range(0, width // 2, 8):
+        sums = tapped(high, taps.at[1], left)
+        for half in range(2):
+            at = slice(left + half * (width // 2), left + half * (width // 2) + 8)
+            part = sums[:, :, half * (D - LANES) : (half + 1) * (D - LANES)]
+            conv[:, at, LANES:] = after[:, at, LANES:] + part
 
     flat = conv[...].reshape(rows * width, D)
-    normed = norm(flat, gain_ref[2]).astype(jnp.bfloat16)
+    normed = norm(flat, gain).astype(jnp.bfloat16)
     up = jnp.dot(normed, up_ref[...], preferred_element_type=jnp.float32)
     hidden = (0.5 * up * (1.0 + lax.erf(up * 0.5**0.5))).astype(jnp.bfloat16)
     outcome = flat + jnp.dot(hidden, down_ref[...], preferred_element_type=jnp.float32)
@@ -201,6 +232,8 @@
     out_ref,
     received,
     wide,
+    low,
+    high,
     taps,
     conv,
     beside,
@@ -221,12 +254,13 @@
     @pl.when(step == 0)
     def _():
         greet(True)
-        taps[...] = jnp.broadcast_to(taps_ref[...][:, None, :], taps.shape)
         exchange(normed_ref, wide, beside, above, corner, halo_send, halo_recv)
-
-    current = mix(step * rows, after_ref, wide, taps, conv, gain_ref, up_ref, down_ref)
+        shift(wide, low, high, taps, taps_ref)
+
+    gain = gain_ref[0, 2:3]
+    current = mix(step * rows, after_ref, low, high, taps, conv, gain, up_ref, down_ref)
     out_ref[...] = current.reshape(rows, width, D)
-    following = norm(current.astype(jnp.float32), gain_ref[3]).reshape(rows, width, D)
+    following = norm(current.astype(jnp.float32), gain_ref[1, 0:1]).reshape(rows, width, D)
 
     for k in range(per_step):
         for pair in range(pairs):
@@ -368,6 +402,8 @@
     after,
     normed,
     wide,
+    low,
+    high,
     taps,
     conv,
     beside,
@@ -382,7 +418,6 @@
 
     @pl.when(step == 0)
     def _():
-        taps[...] = jnp.broadcast_to(taps_ref[...][:, None, :], taps.shape)
 
         @pl.loop(0, row_count * row_repeat)
         def _(chunk):
@@ -395,21 +430,27 @@
                     total = total + packed[:, half * D : (half + 1) * D]
                     after[row] = total
                     normed[row] = (
-                        norm(total, gain_ref[1]).reshape(width // 8, 8, D).astype(jnp.bfloat16)
+                        norm(total, gain_ref[1, 1:2]).reshape(width // 8, 8, D).astype(jnp.bfloat16)
                     )
 
         greet(False)
         exchange(normed, wide, beside, above, corner, halo_send, halo_recv)
+        shift(wide, low, high, taps, taps_ref)
 
     base = step * rows
-    current = mix(
-        base, after.at[pl.ds(base, rows)], wide, taps, conv, gain_ref, up_ref, down_ref
-    )
+    gain = gain_ref[1, 2:3]
+    stripes = after.at[pl.ds(base, rows)]
+    current = mix(base, stripes, low, high, taps, conv, gain, up_ref, down_ref)
     out_ref[...] = current.reshape(rows, width, D)
 
 
 def whole(shape):
     return pl.BlockSpec(shape, lambda i: (0,) * len(shape))
+
+
+def layer_of(array, layer):
+    block = (None,) + array.shape[1:]
+    return pl.BlockSpec(block, lambda i: (layer,) + (0,) * (len(block) - 1))
 
 
 def stripe(width):
@@ -420,7 +461,9 @@
     dma = pltpu.SemaphoreType.DMA
     return [
         pltpu.VMEM((height + 2 * HALO, width + 16, D), jnp.float32),
-        pltpu.VMEM((KS * KS, 8, D), jnp.float32),
+        pltpu.VMEM((KS, height + 2 * HALO, width, LANES), jnp.float32),
+        pltpu.VMEM((KS, height + 2 * HALO, width // 2, LANES), jnp.float32),
+        pltpu.VMEM((2, KS * KS, 8, LANES), jnp.float32),
         pltpu.VMEM((WS, width, D), jnp.float32),
         pltpu.VMEM((2, height, 8, D), jnp.bfloat16),
         pltpu.VMEM((2, HALO, width // 8, 8, D), jnp.bfloat16),
@@ -446,33 +489,29 @@
     moved = jax.ShapeDtypeStruct(
         (row_count, col_count, row_repeat, pairs, col_piece, 2 * D), jnp.bfloat16
     )
-    qkv_parts = qkv_weight.reshape(LAYERS, D, 3, D).transpose(0, 2, 1, 3)
-    biases = [score_bias(bias_table[layer]) for layer in range(LAYERS)]
-    gains = jnp.concatenate([norm_gain, jnp.roll(norm_gain[:, :1], -1, axis=0)], axis=1)
-    gains = gains[:, :, None, :]
-    gain_shape = gains.shape[1:]
-    weight_specs = [
-        whole(gain_shape),
-        whole((KS * KS, D)),
-        whole(up_weight.shape[1:]),
-        whole(down_weight.shape[1:]),
-    ]
-    attention_specs = [whole(qkv_parts.shape[1:]), whole((D, D)), whole(biases[0].shape)]
+    biases = score_biases(bias_table)
+
+    def mix_specs(layer):
+        stacks = (conv_weight, up_weight, down_weight)
+        return [whole(norm_gain.shape)] + [layer_of(stack, layer) for stack in stacks]
+
+    def attention_specs(layer):
+        return [layer_of(stack, layer) for stack in (qkv_weight, proj_weight, biases)]
 
     after, normed_two = pl.pallas_call(
         regular_kernel,
         out_shape=(shape32, shape16),
         grid=(height // WS,),
-        in_specs=[stripe(width), whole(gain_shape)] + attention_specs,
+        in_specs=[stripe(width), whole(norm_gain.shape)] + attention_specs(0),
         out_specs=(stripe(width), stripe(width)),
         name="regular_attention",
-    )(tokens, gains[0], qkv_parts[0], proj_weight[0], biases[0])
+    )(tokens, norm_gain, qkv_weight, proj_weight, biases)
 
     current, received = pl.pallas_call(
         first_mix_kernel,
         out_shape=(shape16, moved),
         grid=(height // WS,),
-        in_specs=[whole(blocked), stripe(width)] + weight_specs,
+        in_specs=[whole(blocked), stripe(width)] + mix_specs(0),
         out_specs=(stripe(width), pl.BlockSpec(memory_space=pl.ANY)),
         scratch_shapes=mix_scratch(height, width)
         + [
@@ -487,10 +526,10 @@
     )(
         normed_two.reshape(blocked),
         after,
-        gains[0],
-        conv_weight[0],
-        up_weight[0],
-        down_weight[0],
+        norm_gain,
+        conv_weight,
+        up_weight,
+        down_weight,
     )
 
     returned = pl.pallas_call(
@@ -503,7 +542,7 @@
                 lambda i: (0, 0, 0, i, 0, 0),
             )
         ]
-        + attention_specs,
+        + attention_specs(1),
         out_specs=pl.BlockSpec(memory_space=pl.ANY),
         scratch_shapes=[
             pltpu.VMEM(
@@ -514,13 +553,13 @@
         ],
         compiler_params=pltpu.CompilerParams(collective_id=1, has_side_effects=True),
         name="shuffle_attention",
-    )(received, qkv_parts[1], proj_weight[1], biases[1])
+    )(received, qkv_weight, proj_weight, biases)
 
     return pl.pallas_call(
         last_mix_kernel,
         out_shape=shape16,
         grid=(height // WS,),
-        in_specs=[whole(tokens.shape), whole(moved.shape)] + weight_specs,
+        in_specs=[whole(tokens.shape), whole(moved.shape)] + mix_specs(1),
         out_specs=stripe(width),
         scratch_shapes=[
             pltpu.VMEM(tokens.shape, jnp.float32),
@@ -529,7 +568,7 @@
         + mix_scratch(height, width),
         compiler_params=pltpu.CompilerParams(collective_id=2, has_side_effects=True),
         name="last_mix",
-    )(current, returned, gains[1], conv_weight[1], up_weight[1], down_weight[1])
+    )(current, returned, norm_gain, conv_weight, up_weight, down_weight)
 
 
 def solution(mesh):

time: 139 us -> 119 us (0.86)
  Pallas kernels: 122 us -> 107 us
  local copies, waits for them, and re-layouts: 11.3 us -> 8.36 us
  matrix products: 3.99 us -> 1.33 us
    pallas_call x1, Pallas kernels: 36.4 us -> 27 us  [on_device(): pl.pallas_call(last_mix_kernel, out_shape=shape16, grid=(height // WS,),...]
    squeeze x5 -> x0, local copies, waits for them, and re-layouts: 3.68 us -> none  [the longest x1 0.86 us: on_device(): up_weight[1]]
    pallas_call x1, Pallas kernels: 43.1 us -> 39.4 us  [on_device(): pl.pallas_call(first_mix_kernel, out_shape=(shape16, moved), grid=(height...]
    unnamed x16 -> x7, local copies, waits for them, and re-layouts: 4.41 us -> 7.07 us
    dot_general x2 -> x1, matrix products: 3.99 us -> 1.33 us  [score_biases(): jnp.dot(tables, selector, precision=lax.Precision.HIGHEST) * LOG2E]
    pallas_call x1, Pallas kernels: 30.8 us -> 28.7 us  [on_device(): pl.pallas_call(shuffle_kernel, out_shape=moved, grid=(pairs,), in_specs=[...]
where the time goes in v2:
time: 119 us; the launch traced here: 117 us
  Pallas kernels  107 us (90%)
  local copies, waits for them, and re-layouts  8.36 us (7%)
  matrix products  1.33 us (1%)
    pallas_call x1, Pallas kernels, on_device(): pl.pallas_call(first_mix_kernel, out_shape=(shape16, moved), grid=(height...  39.4 us
    pallas_call x1, Pallas kernels, on_device(): pl.pallas_call(shuffle_kernel, out_shape=moved, grid=(pairs,), in_specs=[...  28.7 us
    pallas_call x1, Pallas kernels, on_device(): pl.pallas_call(last_mix_kernel, out_shape=shape16, grid=(height // WS,),...  27 us
    pallas_call x1, Pallas kernels, on_device(): pl.pallas_call(regular_kernel, out_shape=(shape32, shape16), grid=(height...  12 us
    unnamed x7, local copies, waits for them, and re-layouts  7.07 us

profile of v2, /device:TPU:1, one launch (start us, length us, event | category | flops | bytes accessed | tf_op | source)
XLA Modules:
  0.0 117.0 jit_solution(17404593531880690031)
XLA Ops:
  0.0 0.0 copy-start
  0.0 1.3 %copy.19.gain_ref = f32[2,3,192]{2,1,0:T(4,128)} copy(f32[2,3,192]{2,0,1:T(2,128)} %param.9) | data formatting | bytes 9216 | tf_op args[1]
  1.4 0.7 copy.17
  2.1 0.1 add_add_fusion
  2.2 0.1 add.55
  2.2 1.6 %copy.21.taps_ref = f32[2,49,192]{2,1,0:T(8,128)} copy(f32[2,49,192]{2,0,1:T(2,128)} %param.13) | data formatting | bytes 150528 | tf_op args[5]
  3.8 1.3 %fusion = f32[12,4096]{1,0:T(8,128)S(1)} fusion(f32[12,225]{1,0:T(8,128)S(1)} %reshape.95, s32[4096]{0:T(1024)S(1)} %add.55), kind=kOutput, calls=%fused_computation.1 | convolution fusion | flops 133681152 | bytes 223792 | tf_op jit(solution)/shard_map/dot_general | solution.py:44
  5.1 0.2 reshape.96
  5.3 0.2 copy.27
  5.5 0.8 reshape.97.bias_ref
  6.3 0.0 copy-done
  6.3 1.2 copy.22.down_ref
  7.5 12.0 %regular_attention.1 = (f32[32,64,192]{2,1,0:T(8,128)}, bf16[32,64,192]{2,1,0:T(8,128)(2,1)}) custom-call(bf16[32,64,192]{2,1,0:T(8,128)(2,1)} %x_ref.1, f32[2,3,192]{2,1,0:T(4,128)} %copy.19.gain_ref, bf16[2,192,576]{2,1,0:T(8,128)(2,1)} %qkv_ref.3, bf16[2,192,192]{2,1,0:T(8,128)(2,1)} %proj_ref.3, f32[2,64,384]{2,1,0:T(8,128)} %reshape.97.bias_ref), custom_call_target="tpu_custom_call" | custom-call | tf_op jit(solution)/shard_map/regular_attention/pallas_call | solution.py:501
  19.5 39.4 %first_mix.1 = (bf16[32,64,192]{2,1,0:T(8,128)(2,1)}, bf16[4,8,2,2,8,384]{5,4,3,2,1,0:T(8,128)(2,1)}) custom-call(bf16[32,8,8,192]{3,2,1,0:T(8,128)(2,1)} %bitcast.8, f32[32,64,192]{2,1,0:T(8,128)} %get-tuple-element.10.after_ref, f32[2,3,192]{2,1,0:T(4,128)} %copy.19.gain_ref, f32[2,49,192]{2,1,0:T(8,128)} %copy.21.taps_ref, bf16[2,192,768]{2,1,0:T(8,128)(2,1)} %up_ref.3, ...), custom_call_target="tpu_custom_call" | custom-call | tf_op jit(solution)/shard_map/first_mix/pallas_call | solution.py:510
  58.9 28.7 %shuffle_attention.1.returned_ref = bf16[4,8,2,2,8,384]{5,4,3,2,1,0:T(8,128)(2,1)} custom-call(bf16[4,8,2,2,8,384]{5,4,3,2,1,0:T(8,128)(2,1)} %get-tuple-element.12.x_ref, bf16[2,192,576]{2,1,0:T(8,128)(2,1)} %qkv_ref.3, bf16[2,192,192]{2,1,0:T(8,128)(2,1)} %proj_ref.3, f32[2,64,384]{2,1,0:T(8,128)} %reshape.97.bias_ref), custom_call_target="tpu_custom_call" | custom-call | tf_op jit(solution)/shard_map/shuffle_attention/pallas_call | solution.py:535
  87.6 27.0 %last_mix.1 = bf16[32,64,192]{2,1,0:T(8,128)(2,1)} custom-call(bf16[32,64,192]{2,1,0:T(8,128)(2,1)} %get-tuple-element.11.current_ref, bf16[4,8,2,2,8,384]{5,4,3,2,1,0:T(8,128)(2,1)} %shuffle_attention.1.returned_ref, f32[2,3,192]{2,1,0:T(4,128)} %copy.19.gain_ref, f32[2,49,192]{2,1,0:T(8,128)} %copy.21.taps_ref, bf16[2,192,768]{2,1,0:T(8,128)(2,1)} %up_ref.3, ...), custom_call_target="tpu_custom_call" | custom-call | tf_op jit(solution)/shard_map/last_mix/pallas_call | solution.py:558
  114.6 2.3 %copy.29 = bf16[32,64,192]{2,1,0:T(8,128)(2,1)} copy(bf16[32,64,192]{2,1,0:T(8,128)(2,1)} %last_mix.1) | data formatting | bytes 1572864
  (2 shorter events, 0.0 us)
Async XLA Ops:
  0.0 6.3 %copy-start = (bf16[2,768,192]{1,2,0:T(8,128)(2,1)S(1)}, bf16[2,768,192]{1,2,0:T(8,128)(2,1)}, u32[]{:S(2)}) copy-start(bf16[2,768,192]{1,2,0:T(8,128)(2,1)} %param.15) | copy-start | bytes 1769476

commit v3 on v2

--- a/solution.py
+++ b/solution.py
@@ -86,7 +86,7 @@
     branch = branch.reshape(width // WS, WS, WS, D).transpose(1, 0, 2, 3).reshape(rows, width, D)
     after = current + branch
     after_ref[...] = after
-    normed_ref[...] = norm(after, gain_ref[0, 1:2]).astype(jnp.bfloat16)
+    normed_ref[...] = norm(after, gain_ref[1, 0:1]).astype(jnp.bfloat16)
 
 
 def greet(everyone):
@@ -175,10 +175,11 @@
         pl.when(there)(copy.wait_send)
 
 
-def shift(wide, low, high, taps, taps_ref):
+def shift(layer, wide, low, high, taps, taps_ref):
     width = low.shape[2]
-    upper = taps_ref[:, LANES:]
-    taps[0] = jnp.broadcast_to(taps_ref[:, :LANES][:, None, :], taps.shape[1:])
+    own = taps_ref[:, layer]
+    upper = own[:, LANES:]
+    taps[0] = jnp.broadcast_to(own[:, :LANES][:, None, :], taps.shape[1:])
     both = jnp.concatenate([upper, upper], axis=-1)
     taps[1] = jnp.broadcast_to(both[:, None, :], taps.shape[1:])
 
@@ -218,8 +219,14 @@
     normed = norm(flat, gain).astype(jnp.bfloat16)
     up = jnp.dot(normed, up_ref[...], preferred_element_type=jnp.float32)
     hidden = (0.5 * up * (1.0 + lax.erf(up * 0.5**0.5))).astype(jnp.bfloat16)
-    outcome = flat + jnp.dot(hidden, down_ref[...], preferred_element_type=jnp.float32)
+    outcome = flat + lax.dot_general(
+        hidden, down_ref[...], (((1,), (1,)), ((), ())), preferred_element_type=jnp.float32
+    )
     return outcome.astype(jnp.bfloat16)
+
+
+def stripe_at(step, count):
+    return (step + lax.axis_index("row")) % count
 
 
 def first_mix_kernel(
@@ -250,17 +257,18 @@
     per_step = rows // (2 * pairs)
     my_row, my_col = lax.axis_index("row"), lax.axis_index("col")
     step = pl.program_id(0)
+    turned = stripe_at(step, pl.num_programs(0))
 
     @pl.when(step == 0)
     def _():
         greet(True)
         exchange(normed_ref, wide, beside, above, corner, halo_send, halo_recv)
-        shift(wide, low, high, taps, taps_ref)
-
-    gain = gain_ref[0, 2:3]
-    current = mix(step * rows, after_ref, low, high, taps, conv, gain, up_ref, down_ref)
+        shift(0, wide, low, high, taps, taps_ref)
+
+    gain = gain_ref[2, 0:1]
+    current = mix(turned * rows, after_ref, low, high, taps, conv, gain, up_ref, down_ref)
     out_ref[...] = current.reshape(rows, width, D)
-    following = norm(current.astype(jnp.float32), gain_ref[1, 0:1]).reshape(rows, width, D)
+    following = norm(current.astype(jnp.float32), gain_ref[0, 1:2]).reshape(rows, width, D)
 
     for k in range(per_step):
         for pair in range(pairs):
@@ -268,7 +276,7 @@
             packed = jnp.concatenate([following[row], following[row + 1]], axis=-1)
             for col in range(col_count):
                 piece = packed[col * col_piece : (col + 1) * col_piece]
-                outgoing[step * per_step + k, col, pair] = piece.astype(jnp.bfloat16)
+                outgoing[turned * per_step + k, col, pair] = piece.astype(jnp.bfloat16)
 
     def remote(chunk, col):
         return pltpu.make_async_remote_copy(
@@ -280,12 +288,11 @@
             device_id_type=MESH,
         )
 
-    for k in range(per_step):
-        chunk = step * per_step + k
-
-        @pl.loop(0, col_count)
-        def _(turn):
-            col = (my_col + turn) % col_count
+    @pl.loop(0, col_count)
+    def _(turn):
+        col = (my_col + turn) % col_count
+        for k in range(per_step):
+            chunk = turned * per_step + k
             mine = (chunk % row_count == my_row) & (col == my_col)
 
             @pl.when(mine)
@@ -369,11 +376,13 @@
             recv_sem.at[pair, row, col],
         )
 
-    @pl.loop(0, row_count)
-    def _(row):
-        @pl.loop(0, col_count)
-        def _(turn):
-            col = (my_col + turn) % col_count
+    @pl.loop(0, col_count)
+    def _(turn):
+        col = (my_col + turn) % col_count
+
+        @pl.loop(0, row_count)
+        def _(row_turn):
+            row = (my_row + row_turn) % row_count
             mine = (row == my_row) & (col == my_col)
             pl.when(mine)(lambda: local(step, row, col).start())
             pl.when(jnp.logical_not(mine))(lambda: remote(step, row, col).start())
@@ -435,10 +444,10 @@
 
         greet(False)
         exchange(normed, wide, beside, above, corner, halo_send, halo_recv)
-        shift(wide, low, high, taps, taps_ref)
+        shift(1, wide, low, high, taps, taps_ref)
 
     base = step * rows
-    gain = gain_ref[1, 2:3]
+    gain = gain_ref[2, 1:2]
     stripes = after.at[pl.ds(base, rows)]
     current = mix(base, stripes, low, high, taps, conv, gain, up_ref, down_ref)
     out_ref[...] = current.reshape(rows, width, D)
@@ -490,10 +499,12 @@
         (row_count, col_count, row_repeat, pairs, col_piece, 2 * D), jnp.bfloat16
     )
     biases = score_biases(bias_table)
+    gains, taps = norm_gain.transpose(1, 0, 2), conv_weight.transpose(1, 0, 2)
+    down_turned = down_weight.transpose(0, 2, 1)
 
     def mix_specs(layer):
-        stacks = (conv_weight, up_weight, down_weight)
-        return [whole(norm_gain.shape)] + [layer_of(stack, layer) for stack in stacks]
+        stacks = (up_weight, down_turned)
+        return [whole(gains.shape), whole(taps.shape)] + [layer_of(x, layer) for x in stacks]
 
     def attention_specs(layer):
         return [layer_of(stack, layer) for stack in (qkv_weight, proj_weight, biases)]
@@ -502,17 +513,18 @@
         regular_kernel,
         out_shape=(shape32, shape16),
         grid=(height // WS,),
-        in_specs=[stripe(width), whole(norm_gain.shape)] + attention_specs(0),
+        in_specs=[stripe(width), whole(gains.shape)] + attention_specs(0),
         out_specs=(stripe(width), stripe(width)),
         name="regular_attention",
-    )(tokens, norm_gain, qkv_weight, proj_weight, biases)
-
+    )(tokens, gains, qkv_weight, proj_weight, biases)
+
+    turned = pl.BlockSpec((WS, width, D), lambda i: (stripe_at(i, height // WS), 0, 0))
     current, received = pl.pallas_call(
         first_mix_kernel,
         out_shape=(shape16, moved),
         grid=(height // WS,),
-        in_specs=[whole(blocked), stripe(width)] + mix_specs(0),
-        out_specs=(stripe(width), pl.BlockSpec(memory_space=pl.ANY)),
+        in_specs=[whole(blocked), turned] + mix_specs(0),
+        out_specs=(turned, pl.BlockSpec(memory_space=pl.ANY)),
         scratch_shapes=mix_scratch(height, width)
         + [
             pltpu.VMEM(
@@ -526,10 +538,10 @@
     )(
         normed_two.reshape(blocked),
         after,
-        norm_gain,
-        conv_weight,
+        gains,
+        taps,
         up_weight,
-        down_weight,
+        down_turned,
     )
 
     returned = pl.pallas_call(
@@ -568,7 +580,7 @@
         + mix_scratch(height, width),
         compiler_params=pltpu.CompilerParams(collective_id=2, has_side_effects=True),
         name="last_mix",
-    )(current, returned, norm_gain, conv_weight, up_weight, down_weight)
+    )(current, returned, gains, taps, up_weight, down_turned)
 
 
 def solution(mesh):

time: 119 us -> 115 us (0.966)
  local copies, waits for them, and re-layouts: 8.36 us -> 4.33 us
    unnamed x7 -> x2, local copies, waits for them, and re-layouts: 7.07 us -> 3.01 us
    pallas_call x1, Pallas kernels: 39.4 us -> 41.6 us  [on_device(): pl.pallas_call(first_mix_kernel, out_shape=(shape16, moved), grid=(height...]
    pallas_call x1, Pallas kernels: 27 us -> 25.7 us  [on_device(): pl.pallas_call(last_mix_kernel, out_shape=shape16, grid=(height // WS,),...]
where the time goes in v3:
time: 115 us; the launch traced here: 113 us
  Pallas kernels  107 us (93%)
  local copies, waits for them, and re-layouts  4.33 us (4%)
  matrix products  1.34 us (1%)
    pallas_call x1, Pallas kernels, on_device(): pl.pallas_call(first_mix_kernel, out_shape=(shape16, moved), grid=(height...  41.6 us
    pallas_call x1, Pallas kernels, on_device(): pl.pallas_call(shuffle_kernel, out_shape=moved, grid=(pairs,), in_specs=[...  28.1 us
    pallas_call x1, Pallas kernels, on_device(): pl.pallas_call(last_mix_kernel, out_shape=shape16, grid=(height // WS,),...  25.7 us
    pallas_call x1, Pallas kernels, on_device(): pl.pallas_call(regular_kernel, out_shape=(shape32, shape16), grid=(height...  12 us
    unnamed x2, local copies, waits for them, and re-layouts  3.01 us

profile of v3, /device:TPU:1, one launch (start us, length us, event | category | flops | bytes accessed | tf_op | source)
XLA Modules:
  0.0 113.1 jit_solution(4847414651924627707)
XLA Ops:
  0.0 0.7 copy.10
  0.7 0.1 add_add_fusion
  0.8 0.1 add.55
  0.9 1.3 %fusion = f32[12,4096]{1,0:T(8,128)S(1)} fusion(f32[12,225]{1,0:T(8,128)S(1)} %reshape.95, s32[4096]{0:T(1024)S(1)} %add.55), kind=kOutput, calls=%fused_computation.1 | convolution fusion | flops 133681152 | bytes 223792 | tf_op jit(solution)/shard_map/dot_general | solution.py:44
  2.2 0.2 reshape.96
  2.4 0.2 copy.13
  2.6 0.8 reshape.97.bias_ref
  3.5 12.0 %regular_attention.1 = (f32[32,64,192]{2,1,0:T(8,128)}, bf16[32,64,192]{2,1,0:T(8,128)(2,1)}) custom-call(bf16[32,64,192]{2,1,0:T(8,128)(2,1)} %x_ref.1, f32[3,2,192]{2,1,0:T(2,128)} %bitcast.16, bf16[2,192,576]{2,1,0:T(8,128)(2,1)} %qkv_ref.3, bf16[2,192,192]{2,1,0:T(8,128)(2,1)} %proj_ref.3, f32[2,64,384]{2,1,0:T(8,128)} %reshape.97.bias_ref), custom_call_target="tpu_custom_call" | custom-call | tf_op jit(solution)/shard_map/regular_attention/pallas_call | solution.py:512
  15.5 41.6 %first_mix.1 = (bf16[32,64,192]{2,1,0:T(8,128)(2,1)}, bf16[4,8,2,2,8,384]{5,4,3,2,1,0:T(8,128)(2,1)}) custom-call(bf16[32,8,8,192]{3,2,1,0:T(8,128)(2,1)} %bitcast.13, f32[32,64,192]{2,1,0:T(8,128)} %get-tuple-element.10.after_ref, f32[3,2,192]{2,1,0:T(2,128)} %bitcast.17, f32[49,2,192]{2,1,0:T(2,128)} %bitcast.14, bf16[2,192,768]{2,1,0:T(8,128)(2,1)} %up_ref.3, ...), custom_call_target="tpu_custom_call" | custom-call | tf_op jit(solution)/shard_map/first_mix/pallas_call | solution.py:522
  57.0 28.1 %shuffle_attention.1.returned_ref = bf16[4,8,2,2,8,384]{5,4,3,2,1,0:T(8,128)(2,1)} custom-call(bf16[4,8,2,2,8,384]{5,4,3,2,1,0:T(8,128)(2,1)} %get-tuple-element.12.x_ref, bf16[2,192,576]{2,1,0:T(8,128)(2,1)} %qkv_ref.3, bf16[2,192,192]{2,1,0:T(8,128)(2,1)} %proj_ref.3, f32[2,64,384]{2,1,0:T(8,128)} %reshape.97.bias_ref), custom_call_target="tpu_custom_call" | custom-call | tf_op jit(solution)/shard_map/shuffle_attention/pallas_call | solution.py:547
  85.2 25.7 %last_mix.1 = bf16[32,64,192]{2,1,0:T(8,128)(2,1)} custom-call(bf16[32,64,192]{2,1,0:T(8,128)(2,1)} %get-tuple-element.11.current_ref, bf16[4,8,2,2,8,384]{5,4,3,2,1,0:T(8,128)(2,1)} %shuffle_attention.1.returned_ref, f32[3,2,192]{2,1,0:T(2,128)} %bitcast.18, f32[49,2,192]{2,1,0:T(2,128)} %bitcast.15, bf16[2,192,768]{2,1,0:T(8,128)(2,1)} %up_ref.3, ...), custom_call_target="tpu_custom_call" | custom-call | tf_op jit(solution)/shard_map/last_mix/pallas_call | solution.py:570
  110.8 2.3 %copy.15 = bf16[32,64,192]{2,1,0:T(8,128)(2,1)} copy(bf16[32,64,192]{2,1,0:T(8,128)(2,1)} %last_mix.1) | data formatting | bytes 1572864
  (2 shorter events, 0.0 us)

commit v4 on v3

--- a/solution.py
+++ b/solution.py
@@ -290,7 +290,7 @@
 
     @pl.loop(0, col_count)
     def _(turn):
-        col = (my_col + turn) % col_count
+        col = (my_col + col_count // 2 + turn) % col_count
         for k in range(per_step):
             chunk = turned * per_step + k
             mine = (chunk % row_count == my_row) & (col == my_col)
@@ -378,7 +378,7 @@
 
     @pl.loop(0, col_count)
     def _(turn):
-        col = (my_col + turn) % col_count
+        col = (my_col + col_count // 2 + turn) % col_count
 
         @pl.loop(0, row_count)
         def _(row_turn):

time: 115 us -> 115 us (level)
  no operation moved by 1% of the time
where the time goes in v4:
time: 115 us; the launch traced here: 114 us
  Pallas kernels  108 us (94%)
  local copies, waits for them, and re-layouts  4.33 us (4%)
  matrix products  1.34 us (1%)
    pallas_call x1, Pallas kernels, on_device(): pl.pallas_call(first_mix_kernel, out_shape=(shape16, moved), grid=(height...  42.2 us
    pallas_call x1, Pallas kernels, on_device(): pl.pallas_call(shuffle_kernel, out_shape=moved, grid=(pairs,), in_specs=[...  27.5 us
    pallas_call x1, Pallas kernels, on_device(): pl.pallas_call(last_mix_kernel, out_shape=shape16, grid=(height // WS,),...  26.3 us
    pallas_call x1, Pallas kernels, on_device(): pl.pallas_call(regular_kernel, out_shape=(shape32, shape16), grid=(height...  12 us
    unnamed x2, local copies, waits for them, and re-layouts  3.01 us

profile of v4, /device:TPU:1, one launch (start us, length us, event | category | flops | bytes accessed | tf_op | source)
XLA Modules:
  0.0 113.8 jit_solution(3907139392939428056)
XLA Ops:
  0.0 0.7 copy.10
  0.7 0.1 add_add_fusion
  0.8 0.1 add.55
  0.9 1.3 %fusion = f32[12,4096]{1,0:T(8,128)S(1)} fusion(f32[12,225]{1,0:T(8,128)S(1)} %reshape.95, s32[4096]{0:T(1024)S(1)} %add.55), kind=kOutput, calls=%fused_computation.1 | convolution fusion | flops 133681152 | bytes 223792 | tf_op jit(solution)/shard_map/dot_general | solution.py:44
  2.2 0.2 reshape.96
  2.4 0.2 copy.13
  2.6 0.8 reshape.97.bias_ref
  3.5 12.0 %regular_attention.1 = (f32[32,64,192]{2,1,0:T(8,128)}, bf16[32,64,192]{2,1,0:T(8,128)(2,1)}) custom-call(bf16[32,64,192]{2,1,0:T(8,128)(2,1)} %x_ref.1, f32[3,2,192]{2,1,0:T(2,128)} %bitcast.16, bf16[2,192,576]{2,1,0:T(8,128)(2,1)} %qkv_ref.3, bf16[2,192,192]{2,1,0:T(8,128)(2,1)} %proj_ref.3, f32[2,64,384]{2,1,0:T(8,128)} %reshape.97.bias_ref), custom_call_target="tpu_custom_call" | custom-call | tf_op jit(solution)/shard_map/regular_attention/pallas_call | solution.py:512
  15.5 42.2 %first_mix.1 = (bf16[32,64,192]{2,1,0:T(8,128)(2,1)}, bf16[4,8,2,2,8,384]{5,4,3,2,1,0:T(8,128)(2,1)}) custom-call(bf16[32,8,8,192]{3,2,1,0:T(8,128)(2,1)} %bitcast.13, f32[32,64,192]{2,1,0:T(8,128)} %get-tuple-element.10.after_ref, f32[3,2,192]{2,1,0:T(2,128)} %bitcast.17, f32[49,2,192]{2,1,0:T(2,128)} %bitcast.14, bf16[2,192,768]{2,1,0:T(8,128)(2,1)} %up_ref.3, ...), custom_call_target="tpu_custom_call" | custom-call | tf_op jit(solution)/shard_map/first_mix/pallas_call | solution.py:522
  57.7 27.5 %shuffle_attention.1.returned_ref = bf16[4,8,2,2,8,384]{5,4,3,2,1,0:T(8,128)(2,1)} custom-call(bf16[4,8,2,2,8,384]{5,4,3,2,1,0:T(8,128)(2,1)} %get-tuple-element.12.x_ref, bf16[2,192,576]{2,1,0:T(8,128)(2,1)} %qkv_ref.3, bf16[2,192,192]{2,1,0:T(8,128)(2,1)} %proj_ref.3, f32[2,64,384]{2,1,0:T(8,128)} %reshape.97.bias_ref), custom_call_target="tpu_custom_call" | custom-call | tf_op jit(solution)/shard_map/shuffle_attention/pallas_call | solution.py:547
  85.2 26.3 %last_mix.1 = bf16[32,64,192]{2,1,0:T(8,128)(2,1)} custom-call(bf16[32,64,192]{2,1,0:T(8,128)(2,1)} %get-tuple-element.11.current_ref, bf16[4,8,2,2,8,384]{5,4,3,2,1,0:T(8,128)(2,1)} %shuffle_attention.1.returned_ref, f32[3,2,192]{2,1,0:T(2,128)} %bitcast.18, f32[49,2,192]{2,1,0:T(2,128)} %bitcast.15, bf16[2,192,768]{2,1,0:T(8,128)(2,1)} %up_ref.3, ...), custom_call_target="tpu_custom_call" | custom-call | tf_op jit(solution)/shard_map/last_mix/pallas_call | solution.py:570
  111.4 2.3 %copy.15 = bf16[32,64,192]{2,1,0:T(8,128)(2,1)} copy(bf16[32,64,192]{2,1,0:T(8,128)(2,1)} %last_mix.1) | data formatting | bytes 1572864
  (2 shorter events, 0.0 us)
